TPU v7x, 512 devices: a whole 4x4x16 slice. The times are simulated.
512 devices in a mesh: sky: 128 (over z, x, core), band: 4 (over y).
Axes of the slice: x: 4, y: 4, z: 16, core: 2. Of those that a mesh axis runs over, the one named last changes fastest.
Arguments:
- tiles: bfloat16 [4, 8192, 32, 256], P('band', 'sky'), may hold values from -6 to 6
- coefs: bfloat16 [4, 8192, 5], P('band', 'sky'), may hold values from -3 to 3
- tile_patch: int32 [4, 8192, 1], P('band', 'sky'), may hold values from 0 to 127; in each aligned block of 64 rows (0 to 63, 64 to 127, ..., all dimensions but the last counted through in order) at most 2 rows name the same one
- tile_offset: int32 [4, 8192], P('band', 'sky'), may hold values from 0 to 32
- weight_index: int32 [4, 8192], P('band', 'sky'), may hold values from 0 to 15
- weight_table: bfloat16 [4, 16], P('band'), may hold values from 0.5 to 2
- taps_rows: bfloat16 [4, 5, 41], P('band'), may hold values from -1 to 1
- taps_cols: bfloat16 [4, 5, 41], P('band'), may hold values from -1 to 1
- gains: float32 [4], P('band'), may hold values from 0.5 to 2
- profiles: bfloat16 [4, 8192, 256], P('band', 'sky'), may hold values from -0.375 to 0.375
- source_patch: int32 [4, 8192, 1], P('band', 'sky'), may hold values from 0 to 127; in each aligned block of 64 rows (0 to 63, 64 to 127, ..., all dimensions but the last counted through in order) at most 2 rows name the same one
- source_row: int32 [4, 8192], P('band', 'sky'), may hold values from 0 to 63
Outputs:
- coadded: float32 [4, 8192, 256], P('band', 'sky')
- detection: float32 [8192, 256], P('sky')
- fluxes: float32 [4, 8192], P('band', 'sky')
Inputs may be any that keep to these rules, and one draw needn't show every extreme that they name: `tile_patch`: in the strips of one device at most 2 go to one patch. `source_patch`: in the sources of one device at most 2 go to one patch.
All inputs are finite; a program needn't handle non-finite values.
Results may differ from a plain program's by a relative error of at most 0.0041.
Values may be sent and summed in bfloat16 or wider, within the bound.
No kernel may reach another device: no remote copies, remote signals or barrier semaphores. Data moves between devices by JAX's collectives and lax.ppermute only.
A program may use at most 64 MiB of HBM per device.

v0:
```python
import jax
import jax.numpy as jnp
from jax import lax
from jax.sharding import PartitionSpec as P


def in_one_piece(arrays, axis, split_dim, concat_dim, along):
    columns = [a.reshape(*a.shape[:along], -1) for a in arrays]
    both = jnp.concatenate(columns, axis=along)
    out, at, gathered = (
        lax.all_to_all(both, axis, split_axis=split_dim, concat_axis=concat_dim, tiled=True),
        0,
        [],
    )
    for a, column in zip(arrays, columns):
        piece = out[..., at : at + column.shape[along]]
        gathered.append(piece.reshape(*piece.shape[:along], *a.shape[along:]))
        at += column.shape[along]
    return tuple(gathered)


def sent_together(arrays, axis, split_dim, concat_dim, along):
    both = jnp.concatenate(arrays, axis=along)
    out, at, gathered = (
        lax.all_to_all(both, axis, split_axis=split_dim, concat_axis=concat_dim, tiled=True),
        0,
        [],
    )
    for a in arrays:
        gathered.append(lax.slice_in_dim(out, at, at + a.shape[along], axis=along))
        at += a.shape[along]
    return tuple(gathered)


def sent_to_all(value, axis):
    copies = jnp.broadcast_to(value, (lax.axis_size(axis), *value.shape))
    return lax.all_to_all(copies, axis, split_axis=0, concat_axis=0, tiled=True)


def taken_together(value, axis):
    everything = sent_to_all(value, axis)
    return jnp.sum(everything, axis=0)


def band_matrix(taps, size):
    tap_total = taps.shape[1]
    half_width = (tap_total - 1) // 2
    row_ids = jnp.arange(size, dtype=jnp.int32)[:, None]
    col_ids = jnp.arange(size, dtype=jnp.int32)[None, :]
    offset_lag = row_ids - col_ids + half_width
    lag_ids = jnp.arange(tap_total, dtype=jnp.int32)
    lag_table = (offset_lag[:, :, None] == lag_ids[None, None, :]).astype(taps.dtype)
    built = jnp.einsum("ijd,kd->kij", lag_table, taps, preferred_element_type=jnp.float32)
    return built.astype(taps.dtype)


def match_tiles(pixels, weights_k, vertical, horizontal):
    across = jnp.einsum("nij,kjl->nkil", pixels, horizontal, preferred_element_type=jnp.float32)
    across = (across * weights_k.astype(jnp.float32)[:, :, None, None]).astype(jnp.bfloat16)
    matched = jnp.einsum("kia,nkal->nil", vertical, across, preferred_element_type=jnp.float32)
    return matched.astype(jnp.bfloat16)


def match_blocks(pixels, weights_k, vertical, horizontal):
    row_total = pixels.shape[0]
    block_rows = 32
    grouped = (
        pixels.reshape(row_total // block_rows, block_rows, pixels.shape[1], pixels.shape[2]),
        weights_k.reshape(row_total // block_rows, block_rows, weights_k.shape[1]),
    )

    def one_block(pair):
        return match_tiles(pair[0], pair[1], vertical, horizontal)

    return lax.map(one_block, grouped).reshape(pixels.shape)


def slot_of(targets, capacity):
    row_total = targets.shape[0]
    positions = jnp.arange(row_total, dtype=jnp.int32)
    matching = targets[:, None] == targets[None, :]
    earlier = positions[None, :] < positions[:, None]
    ranking = jnp.sum(jnp.where(matching & earlier, 1, 0), axis=1).astype(jnp.int32)
    return targets * capacity + ranking


def place_rows(slots, slot_total, values):
    one_hot = (jnp.arange(slot_total, dtype=jnp.int32)[:, None] == slots[None, :]).astype(
        jnp.bfloat16
    )
    return jnp.dot(one_hot, values, preferred_element_type=jnp.float32).astype(jnp.bfloat16)


def per_device(
    tiles,
    coefs,
    tile_patch,
    tile_offset,
    weight_index,
    weight_table,
    taps_rows,
    taps_cols,
    gains,
    profiles,
    source_patch,
    source_row,
):
    sky_count = lax.axis_size("sky")
    tile_rows = tiles.shape[2]
    tile_cols = tiles.shape[3]
    canvas_rows = 2 * tile_rows
    tile_total = tiles.shape[1]
    source_total = profiles.shape[1]
    capacity = max(2, 2 * tile_total // sky_count)
    source_capacity = max(2, 2 * source_total // sky_count)
    vertical = band_matrix(taps_rows[0], tile_rows)
    horizontal = jnp.transpose(band_matrix(taps_cols[0], tile_cols), (0, 2, 1))
    slot_index = slot_of(tile_patch[0, :, 0], capacity)
    visit_ids = jnp.arange(weight_table.shape[1], dtype=jnp.int32)
    weight = jnp.sum(
        jnp.where(
            weight_index[0][:, None] == visit_ids[None, :],
            weight_table[0][None, :].astype(jnp.float32),
            0.0,
        ),
        axis=1,
    ).astype(jnp.bfloat16)
    offset_value = tile_offset[0].astype(jnp.bfloat16)
    payload = match_blocks(tiles[0], coefs[0], vertical, horizontal)
    details = jnp.stack([weight, offset_value], axis=1)
    slot_total = sky_count * capacity
    send_tiles = place_rows(
        slot_index, slot_total, payload.reshape(tile_total, tile_rows * tile_cols)
    ).reshape(slot_total, tile_rows, tile_cols)
    send_details = place_rows(slot_index, slot_total, details)
    source_slot = slot_of(source_patch[0, :, 0], source_capacity)
    source_slots_all = sky_count * source_capacity
    send_profiles = place_rows(source_slot, source_slots_all, profiles[0])
    send_rows = place_rows(
        source_slot, source_slots_all, source_row[0].astype(jnp.bfloat16)[:, None]
    )
    got_tiles, got_details = in_one_piece((send_tiles, send_details), "sky", 0, 0, 1)
    got_profiles, got_rows = sent_together((send_profiles, send_rows), "sky", 0, 0, 1)
    got_weight = got_details[:, -2]
    got_offset = got_details[:, -1].astype(jnp.int32)
    row_index = got_offset[:, None] + jnp.arange(tile_rows, dtype=jnp.int32)[None, :]
    canvas_ids = jnp.arange(canvas_rows, dtype=jnp.int32)
    placed = canvas_ids[None, :, None] == row_index[:, None, :]
    placed_weight = jnp.where(placed, got_weight[:, None, None], jnp.zeros((), jnp.bfloat16))
    numerator = jnp.einsum(
        "nri,nil->rl", placed_weight, got_tiles, preferred_element_type=jnp.float32
    )
    coverage = jnp.sum(placed_weight.astype(jnp.float32), axis=(0, 2))
    coadded = numerator / jnp.maximum(coverage, 1.0)[:, None]
    detection = taken_together(gains[0] * coadded, "band")
    row_pick = (got_rows[:, 0].astype(jnp.int32)[:, None] == canvas_ids[None, :]).astype(
        jnp.float32
    )
    picked = jnp.dot(
        row_pick, detection, precision=lax.Precision.HIGHEST, preferred_element_type=jnp.float32
    )
    measured = jnp.sum(got_profiles.astype(jnp.float32) * picked, axis=1)
    returned = lax.all_to_all(measured[:, None], "sky", split_axis=0, concat_axis=0, tiled=True)
    back_pick = (
        source_slot[:, None] == jnp.arange(source_slots_all, dtype=jnp.int32)[None, :]
    ).astype(jnp.float32)
    fluxes = jnp.dot(
        back_pick, returned, precision=lax.Precision.HIGHEST, preferred_element_type=jnp.float32
    )[:, 0]
    return (coadded[None], detection, fluxes[None])


def solution(mesh):
    return jax.shard_map(
        per_device,
        mesh=mesh,
        in_specs=(
            P("band", "sky", None, None),
            P("band", "sky", None),
            P("band", "sky", None),
            P("band", "sky"),
            P("band", "sky"),
            P("band", None),
            P("band", None, None),
            P("band", None, None),
            P("band"),
            P("band", "sky", None),
            P("band", "sky", None),
            P("band", "sky"),
        ),
        out_specs=(P("band", "sky", None), P("sky", None), P("band", "sky")),
        check_vma=False,
    )
```

profile of v0, /device:TPU:1, one launch (start us, length us, event | category | flops | bytes accessed | tf_op | source)
XLA Modules:
  0.0 319.3 jit_solution(7588541235666157542)
XLA Ops:
  0.7 0.9 select_reduce_fusion.1
  2.3 3.2 fusion.31
  6.9 4.8 %while.10 = (s32[]{:T(128)}, bf16[2,32,32,256]{3,2,1,0:T(8,128)(2,1)S(1)}, bf16[2,32,32,256]{3,2,1,0:T(8,128)(2,1)}, bf16[5,256,256]{2,1,0:T(8,128)(2,1)S(1)}, b...) while((s32[]{:T(128)}, bf16[2,32,32,256]{3,2,1,0:T(8,128)(2,1)S(1)}, ...), condition=%wide.region_2.3_spmd, body=%wide.region_1.2_spmd.sunk | while | flops 757858496 | bytes 1763345 | solution.py:75
  6.9 2.4 fusion.79
  9.3 2.4 fusion.79
  12.3 3.2 %convolution_convert_fusion = bf16[256,8192]{1,0:T(8,128)(2,1)} fusion(bf16[64,8192]{1,0:T(8,128)(2,1)S(1)} %bitcast.111, s32[64]{0:T(128)S(1)} %multiply_add_fusion.1), kind=kOutput, calls=%fused_computation.17 | convolution fusion | flops 270548992 | bytes 5243136 | tf_op jit(solution)/shard_map/dot_general | solution.py:91
  15.9 4.5 %pad_maximum_fusion = bf16[256,8194]{1,0:T(8,128)(2,1)} fusion(bf16[256,2]{1,0:T(8,128)(2,1)S(1)} %copy.57, bf16[256,8192]{1,0:T(8,128)(2,1)} %convolution_convert_fusion), kind=kLoop, calls=%fused_computation.19 | loop fusion | flops 8390656 | bytes 8390656 | tf_op jit(solution)/shard_map/concatenate | solution.py:9
  20.4 7.3 %all_to_all.23 = bf16[128,2,8194]{2,1,0:T(2,128)(2,1)} reshape(bf16[256,8194]{1,0:T(8,128)(2,1)} %pad_maximum_fusion) | data formatting | bytes 8390656 | tf_op jit(solution)/shard_map/all_to_all | solution.py:11
  27.7 20.9 %all-to-all-start = ((bf16[128,2,8194]{2,1,0:T(2,128)(2,1)}), bf16[128,2,8194]{2,1,0:T(2,128)(2,1)}, u32[]{:S(2)}, u32[]{:S(2)}) async-start(bf16[128,2,8194]{2,1,0:T(2,128)(2,1)} %all_to_all.23), calls=%async_computation | async-start | bytes 8519680 | tf_op jit(solution)/shard_map/all_to_all | solution.py:11
  50.1 0.9 pad_maximum_fusion.1
  51.0 183.7 %all-to-all-done = bf16[128,2,8194]{2,1,0:T(2,128)(2,1)} async-done(((bf16[128,2,8194]{2,1,0:T(2,128)(2,1)}), bf16[128,2,8194]{2,1,0:T(2,128)(2,1)}, u32[]{:S(2)}, u32[]{:S(2)}) %all-to-all-start) | async-done | bytes 4195360 | tf_op jit(solution)/shard_map/all_to_all | solution.py:11
  234.7 13.4 %all-to-all-start.2 = ((bf16[128,2,257]{2,1,0:T(2,128)(2,1)}), bf16[128,2,257]{2,1,0:T(2,128)(2,1)S(1)}, u32[]{:S(2)}, u32[]{:S(2)}) async-start(bf16[128,2,257]{2,1,0:T(2,128)(2,1)} %pad_maximum_fusion.1), calls=%async_computation.2 | async-start | bytes 393216 | tf_op jit(solution)/shard_map/all_to_all | solution.py:25
  248.1 8.0 %all_to_all.25 = bf16[256,8194]{1,0:T(8,128)(2,1)} reshape(bf16[128,2,8194]{2,1,0:T(2,128)(2,1)} %all-to-all-done) | data formatting | bytes 8390656 | tf_op jit(solution)/shard_map/all_to_all | solution.py:11
  256.1 1.0 convert_reduce_fusion.2
  257.1 1.0 slice_reduce_fusion
  258.1 4.6 %slice.25 = bf16[256,8192]{1,0:T(8,128)(2,1)} slice(bf16[256,8194]{1,0:T(8,128)(2,1)} %all_to_all.25), slice={[0:256], [0:8192]} | slice | bytes 8388608 | tf_op jit(solution)/shard_map/slice | solution.py:16
  262.6 6.4 %copy.58 = bf16[256,8192]{0,1:T(8,128)(2,1)} copy(bf16[256,8192]{1,0:T(8,128)(2,1)} %slice.25) | data formatting | bytes 8388608 | tf_op jit(solution)/shard_map/slice | solution.py:16
  269.3 4.2 %broadcast_multiply_fusion = (f32[64,256]{1,0:T(8,128)S(1)}, f32[64,256]{1,0:T(8,128)}) fusion(f32[]{:T(128)} %bitcast.109, f32[64]{0:T(128)S(1)} %broadcast_maximum_fusion, bf16[256,32,256]{0,2,1:T(8,128)(2,1)} %bitcast.110, s32[256,32]{0,1:T(8,128)S(1)} %iota_add_fusion, bf16[256]{0:T(256)(128)(2,1)S(1)} %slice_reduce_fusion), kind=kOutput, calls=%fused_computation.58 | convolution fusion | flops 269516800 | bytes 4358916 | tf_op jit(solution)/shard_map/nri,nil->rl/dot_general | solution.py:150
  273.6 0.7 broadcast_in_dim.98
  274.3 4.2 %all-to-all-start.1 = ((f32[4,64,256]{2,1,0:T(8,128)}), f32[4,64,256]{2,1,0:T(8,128)S(1)}, u32[]{:S(2)}, u32[]{:S(2)}) async-start(f32[4,64,256]{2,1,0:T(8,128)} %broadcast_in_dim.98), calls=%async_computation.1 | async-start | bytes 524288 | tf_op jit(solution)/shard_map/all_to_all | solution.py:37
  278.9 5.1 %all-to-all-done.1 = f32[4,64,256]{2,1,0:T(8,128)S(1)} async-done(((f32[4,64,256]{2,1,0:T(8,128)}), f32[4,64,256]{2,1,0:T(8,128)S(1)}, u32[]{:S(2)}, u32[]{:S(2)}) %all-to-all-start.1) | async-done | bytes 262176 | tf_op jit(solution)/shard_map/all_to_all | solution.py:37
  284.5 32.5 %all_to_all.35 = f32[128,2,1]{1,2,0:T(1,128)S(1)} all-to-all(f32[128,2,1]{1,2,0:T(1,128)S(1)} %bitcast.113), channel_id=1, replica_groups=mesh['sky'=128,'band'=4] {'sky'}, dimensions={0} | all-to-all | bytes 2048 | tf_op jit(solution)/shard_map/all_to_all | solution.py:163
  317.6 0.8 reduce.9
  318.5 0.7 fusion.52
  (54 shorter events, 5.9 us)
Async XLA Ops:
  0.6 48.9 %copy-start = (bf16[1,64,256]{2,1,0:T(8,128)(2,1)S(1)}, bf16[1,64,256]{2,1,0:T(8,128)(2,1)}, u32[]{:S(2)}) copy-start(bf16[1,64,256]{2,1,0:T(8,128)(2,1)} %param.23) | copy-start | bytes 98308
  0.6 5.6 %copy-start.3 = (bf16[1,5,41]{2,1,0:T(8,128)(2,1)S(1)}, bf16[1,5,41]{2,1,0:T(8,128)(2,1)}, u32[]{:S(2)}) copy-start(bf16[1,5,41]{2,1,0:T(8,128)(2,1)} %param.20) | copy-start | bytes 1234
  0.7 6.1 %copy-start.2 = (bf16[1,64,5]{1,2,0:T(8,128)(2,1)S(1)}, bf16[1,64,5]{1,2,0:T(8,128)(2,1)}, u32[]{:S(2)}) copy-start(bf16[1,64,5]{1,2,0:T(8,128)(2,1)} %param.15) | copy-start | bytes 1924
  6.9 5.4 %copy-start.4 = (bf16[1,16]{1,0:T(2,128)(2,1)S(1)}, bf16[1,16]{1,0:T(2,128)(2,1)}, u32[]{:S(2)}) copy-start(bf16[1,16]{1,0:T(2,128)(2,1)} %param.19) | copy-start | bytes 100
  6.9 5.5 %copy-start.5 = (s32[1,64]{1,0:T(1,128)S(1)}, s32[1,64]{1,0:T(1,128)}, u32[]{:S(2)}) copy-start(s32[1,64]{1,0:T(1,128)} %param.17) | copy-start | bytes 772
  11.7 3.9 %copy-start.6 = (s32[1,64]{1,0:T(1,128)S(1)}, s32[1,64]{1,0:T(1,128)}, u32[]{:S(2)}) copy-start(s32[1,64]{1,0:T(1,128)} %param.18) | copy-start | bytes 772
  27.7 21.6 %copy-start.7 = (s32[1,64,1]{1,2,0:T(1,128)S(1)}, s32[1,64,1]{1,2,0:T(1,128)}, u32[]{:S(2)}) copy-start(s32[1,64,1]{1,2,0:T(1,128)} %param.24) | copy-start | bytes 772
  27.7 22.0 %copy-start.8 = (s32[1,64]{1,0:T(1,128)S(1)}, s32[1,64]{1,0:T(1,128)}, u32[]{:S(2)}) copy-start(s32[1,64]{1,0:T(1,128)} %param.25) | copy-start | bytes 772
  27.7 207.0 %all-to-all-start = ((bf16[128,2,8194]{2,1,0:T(2,128)(2,1)}), bf16[128,2,8194]{2,1,0:T(2,128)(2,1)}, u32[]{:S(2)}, u32[]{:S(2)}) async-start(bf16[128,2,8194]{2,1,0:T(2,128)(2,1)} %all_to_all.23), calls=%async_computation | async-start | bytes 8519680 | tf_op jit(solution)/shard_map/all_to_all | solution.py:11
  234.7 38.8 %all-to-all-start.2 = ((bf16[128,2,257]{2,1,0:T(2,128)(2,1)}), bf16[128,2,257]{2,1,0:T(2,128)(2,1)S(1)}, u32[]{:S(2)}, u32[]{:S(2)}) async-start(bf16[128,2,257]{2,1,0:T(2,128)(2,1)} %pad_maximum_fusion.1), calls=%async_computation.2 | async-start | bytes 393216 | tf_op jit(solution)/shard_map/all_to_all | solution.py:25
  274.3 9.7 %all-to-all-start.1 = ((f32[4,64,256]{2,1,0:T(8,128)}), f32[4,64,256]{2,1,0:T(8,128)S(1)}, u32[]{:S(2)}, u32[]{:S(2)}) async-start(f32[4,64,256]{2,1,0:T(8,128)} %broadcast_in_dim.98), calls=%async_computation.1 | async-start | bytes 524288 | tf_op jit(solution)/shard_map/all_to_all | solution.py:37
  284.0 35.3 %copy-start.1 = (f32[64,256]{1,0:T(8,128)}, f32[64,256]{1,0:T(8,128)S(1)}, u32[]{:S(2)}) copy-start(f32[64,256]{1,0:T(8,128)S(1)} %reduce_sum.57) | copy-start | bytes 196612
where the time goes:
time: 320 us; the launch traced here: 319 us
  waiting for transfers between devices  189 us (59%)
  starting transfers between devices  38.5 us (12%)
  blocking collectives  32.5 us (10%)
  local copies, waits for them, and re-layouts  30.9 us (10%)
  matrix products  17.4 us (5%)
  other arithmetic  9.59 us (3%)
    all_to_all x1, waiting for transfers between devices, in_one_piece(): lax.all_to_all(both, axis, split_axis=split_dim, concat_axis=concat_dim,...  184 us
    all_to_all x1, blocking collectives, per_device(): lax.all_to_all(measured[:, None], 'sky', split_axis=0, concat_axis=0, til...  32.5 us
    all_to_all x1, starting transfers between devices, in_one_piece(): lax.all_to_all(both, axis, split_axis=split_dim, concat_axis=concat_dim,...  20.9 us
    all_to_all x2, local copies, waits for them, and re-layouts, in_one_piece(): lax.all_to_all(both, axis, split_axis=split_dim, concat_axis=concat_dim,...  15.3 us
    all_to_all x1, starting transfers between devices, sent_together(): lax.all_to_all(both, axis, split_axis=split_dim, concat_axis=concat_dim,...  13.4 us
    slice x2, local copies, waits for them, and re-layouts, in_one_piece(): piece = out[..., at:at + column.shape[along]]  10.9 us
  transfers between devices with their start and end apart: 3, of which 2 were waited for; matrix products, arithmetic and copies ran while one was open for 6% of the time, Pallas kernels for 0%

commit v1 on v0

v1 whole, which is shorter than its diff:
```python
import jax
import jax.numpy as jnp
from jax import lax
from jax.experimental import pallas as pl
from jax.experimental.pallas import tpu as pltpu
from jax.sharding import PartitionSpec as P

F32 = jnp.float32
BF16 = jnp.bfloat16
I32 = jnp.int32
NT = (((1,), (1,)), ((), ()))


def iota(shape, dim):
    return lax.broadcasted_iota(I32, shape, dim)


def as_column(row):
    n = row.shape[1]
    eye = iota((n, n), 0) == iota((n, n), 1)
    return jnp.sum(jnp.where(eye, jnp.broadcast_to(row, (n, n)), jnp.zeros_like(row)), axis=1, keepdims=True)


def ranks(patch):
    n = patch.shape[1]
    column = as_column(patch)
    same = (column == patch) & (iota((n, n), 0) < iota((n, n), 1))
    return jnp.sum(same.astype(I32), axis=0, keepdims=True)


def one_hots(patch, total):
    rank = ranks(patch)
    named = iota((total, patch.shape[1]), 0) == patch
    return named & (rank == 0), named & (rank == 1)


def payload_kernel(tp_ref, to_ref, wi_ref, wt_ref, prof_ref, sp_ref, sr_ref, meta_ref, out_ref, stage):
    total = out_ref.shape[0]
    n = tp_ref.shape[1]
    patch = tp_ref[...]
    offset = to_ref[...]
    visits = wt_ref.shape[1]
    visit_hot = iota((visits, n), 0) == wi_ref[...]
    table = as_column(wt_ref[...].astype(F32))
    weight = jnp.sum(jnp.where(visit_hot, table, 0.0), axis=0, keepdims=True)
    meta_ref[0:1, :] = patch
    meta_ref[1:2, :] = offset
    meta_ref[2:3, :] = (weight * 256.0).astype(I32)
    lane = iota((n, 128), 1)
    off_col = as_column(offset.astype(F32))
    w_col = as_column(weight)
    tile_info = jnp.where(lane == 1, off_col, jnp.where(lane == 2, w_col, 0.0)).astype(BF16)
    row_col = as_column(sr_ref[...].astype(F32))
    src_info = jnp.where(lane == 0, row_col, 0.0).astype(BF16)
    tile_hots = one_hots(patch, total)
    src_hots = one_hots(sp_ref[...], total)
    prof = prof_ref[...]
    for s in range(2):
        hot = src_hots[s].astype(F32).astype(BF16)
        sent = jnp.dot(hot, prof, preferred_element_type=F32)
        stage[:, 2 * s, :] = sent[:, :128]
        stage[:, 2 * s + 1, :] = sent[:, 128:]
        thot = tile_hots[s].astype(F32).astype(BF16)
        stage[:, 4 + s, :] = jnp.dot(hot, src_info, preferred_element_type=F32) + jnp.dot(
            thot, tile_info, preferred_element_type=F32
        )
        stage[:, 6 + s, :] = jnp.zeros((total, 128), F32)
    out_ref[...] = stage[...].astype(BF16)


def match_kernel(tiles_ref, coef_ref, tr_ref, tc_ref, out_ref, taps_s, v_s, u_s, ce_s, a_s):
    basis, tap_total = tc_ref.shape
    half = (tap_total - 1) // 2
    cols = tiles_ref.shape[1]
    th = out_ref.shape[1]
    group = 256 // th
    taps_s[...] = jnp.zeros(taps_s.shape, F32)
    taps_s[0:basis, 0:tap_total] = tc_ref[...].astype(F32)
    taps_s[8 : 8 + basis, 0:tap_total] = tr_ref[...].astype(F32)
    taps_s[...] = pltpu.roll(taps_s[...], cols - half, 1)
    lag = iota((cols, cols), 1) - iota((cols, cols), 0)
    inside = (lag >= -half) & (lag <= half)
    for k in range(basis):
        rows = jnp.broadcast_to(taps_s[k : k + 1, :], (cols, cols))
        rolled = pltpu.roll(rows, 0, 1, stride=1, stride_axis=0)
        v_s[k] = jnp.where(inside, rolled, 0.0).astype(BF16)
    parts = []
    for k in range(basis):
        rows = jnp.broadcast_to(taps_s[8 + k : 9 + k, :], (th, cols))
        rolled = pltpu.roll(rows, 0, 1, stride=1, stride_axis=0)
        parts.append(jnp.where(inside[0:th, :], rolled, 0.0)[:, 0:128])
    parts.append(jnp.zeros((256 - basis * th, 128), F32))
    vertical = jnp.concatenate(parts, axis=0).T
    u_s[...] = vertical[0:th, 0 : basis * th].astype(BF16)
    n = coef_ref.shape[1]
    spread = (iota((n * th, n), 0) // th == iota((n * th, n), 1)).astype(F32).astype(BF16)
    ce_s[:, 0:basis] = lax.dot_general(spread, coef_ref[...], NT, preferred_element_type=F32)

    def one_group(g, carry):
        start = pl.multiple_of(g * 256, 256)
        pixels = tiles_ref[pl.ds(start, 256), :]
        coef = ce_s[pl.ds(start, 256), :]
        for k in range(basis):
            across = jnp.dot(pixels, v_s[k], preferred_element_type=F32)
            across = (across * coef[:, k : k + 1]).astype(BF16)
            a_s[:, k * th : (k + 1) * th, :] = across.reshape(group, th, cols)
        for t in range(group):
            done = jnp.dot(u_s[...], a_s[t], preferred_element_type=F32)
            out_ref[g * group + t] = done.astype(BF16)
        return carry

    lax.fori_loop(0, n // group, one_group, 0)


def place_kernel(core_ref, mine_ref, other_ref, m_ref, o_ref, out_ref, canvas):
    core = core_ref[0]
    th = m_ref.shape[1]
    canvas[...] = jnp.zeros(canvas.shape, F32)
    zs = canvas.shape[0] // 4

    for meta, strips in ((mine_ref, m_ref), (other_ref, o_ref)):

        def one_strip(t, carry, meta=meta, strips=strips):
            patch = meta[0, t]

            @pl.when((patch & 1) == core)
            def _():
                q = patch >> 1
                at = (q & 3) * zs + (q >> 2)
                off = meta[1, t]
                w = meta[2, t].astype(F32) * (1.0 / 256.0)
                strip = strips[t].astype(F32) * w
                for h in range(canvas.shape[1]):
                    canvas[at, h, pl.ds(off, th), :] += strip[:, h * 128 : (h + 1) * 128]

            return carry

        lax.fori_loop(0, strips.shape[0], one_strip, 0)
    for h in range(canvas.shape[1]):
        out_ref[:, :, h * 128 : (h + 1) * 128] = canvas[:, h].astype(BF16)


def coadd_kernel(parts_ref, got_ref, gain_ref, out_ref, scaled_ref):
    rows, cols = out_ref.shape
    numerator = jnp.sum(parts_ref[...].astype(F32), axis=0)
    info = got_ref[...].astype(F32)
    total = got_ref.shape[0]
    ids = iota((total, rows), 1).astype(F32)
    coverage = jnp.zeros((1, rows), F32)
    for s in range(2):
        details = info[:, 4 + s, :]
        off, w = details[:, 1:2], details[:, 2:3]
        covered = (ids >= off) & (ids < off + rows // 2)
        coverage = coverage + jnp.sum(jnp.where(covered, w, 0.0), axis=0, keepdims=True)
    column = as_column(jnp.maximum(coverage, 1.0))
    coadded = numerator / column
    out_ref[...] = coadded
    scaled_ref[...] = jnp.broadcast_to((gain_ref[0] * coadded)[None], scaled_ref.shape)


def measure_kernel(bands_ref, got_ref, det_ref, out_ref):
    detection = jnp.sum(bands_ref[...], axis=0)
    det_ref[...] = detection
    info = got_ref[...].astype(F32)
    total = got_ref.shape[0]
    rows = det_ref.shape[0]
    ids = iota((total, rows), 1).astype(F32)
    results = []
    for s in range(2):
        prof = jnp.concatenate([info[:, 2 * s, :], info[:, 2 * s + 1, :]], axis=1)
        row = info[:, 4 + s, 0:1]
        each = lax.dot_general(prof, detection, NT, precision=lax.Precision.HIGHEST, preferred_element_type=F32)
        results.append(jnp.sum(jnp.where(ids == row, each, 0.0), axis=1, keepdims=True))
    lane = iota(out_ref.shape, 1)
    out_ref[...] = jnp.where(lane == 0, results[0], results[1])


def pick_kernel(back_ref, sp_ref, out_ref):
    hots = one_hots(sp_ref[...], back_ref.shape[0])
    back = back_ref[...]
    out_ref[...] = jnp.sum(
        jnp.where(hots[0], back[:, 0:1], 0.0) + jnp.where(hots[1], back[:, 1:2], 0.0), axis=0, keepdims=True
    )


VM = pl.BlockSpec(memory_space=pltpu.VMEM)
SM = pl.BlockSpec(memory_space=pltpu.SMEM)
SDS = jax.ShapeDtypeStruct


def exchange(value, groups=None, axis="sky"):
    return lax.all_to_all(value, axis, split_axis=0, concat_axis=0, tiled=True, axis_index_groups=groups)


def per_device(
    tiles, coefs, tile_patch, tile_offset, weight_index, weight_table,
    taps_rows, taps_cols, gains, profiles, source_patch, source_row,
):
    sky = lax.axis_size("sky")
    band = lax.axis_size("band")
    _, n, th, cols = tiles.shape
    rows = 2 * th
    basis = coefs.shape[2]
    zs = sky // 8
    x_groups = [[(z * 4 + x) * 2 + c for x in range(4)] for z in range(zs) for c in range(2)]
    z_groups = [[(z * 4 + x) * 2 + c for z in range(zs)] for x in range(4) for c in range(2)]
    partners = [(i, i ^ 1) for i in range(sky)]
    core = (lax.axis_index("sky") % 2).astype(I32)[None]

    meta, payload = pl.pallas_call(
        payload_kernel,
        out_shape=(SDS((3, n), I32), SDS((sky, 8, 128), BF16)),
        in_specs=[VM] * 7,
        out_specs=(VM, VM),
        scratch_shapes=[pltpu.VMEM((sky, 8, 128), F32)],
        name="payload",
    )(
        tile_patch[:, :, 0], tile_offset, weight_index, weight_table,
        profiles[0], source_patch[:, :, 0], source_row,
    )
    other_meta = lax.ppermute(meta, "sky", partners)

    matched = pl.pallas_call(
        match_kernel,
        out_shape=SDS((n, th, cols), BF16),
        in_specs=[VM] * 4,
        out_specs=VM,
        scratch_shapes=[
            pltpu.VMEM((16, cols), F32),
            pltpu.VMEM((basis, cols, cols), BF16),
            pltpu.VMEM((th, basis * th), BF16),
            pltpu.VMEM((n * th, 8), F32),
            pltpu.VMEM((256 // th, basis * th, cols), BF16),
        ],
        name="match",
    )(tiles.reshape(n * th, cols), coefs[0].T, taps_rows[0], taps_cols[0])
    other = lax.ppermute(matched, "sky", partners)

    canvas = pl.pallas_call(
        place_kernel,
        out_shape=SDS((sky // 2, rows, cols), BF16),
        in_specs=[SM, SM, SM, VM, VM],
        out_specs=VM,
        scratch_shapes=[pltpu.VMEM((sky // 2, cols // 128, rows, 128), F32)],
        name="place",
    )(core, meta, other_meta, matched, other)

    along_x = exchange(canvas, x_groups).reshape(4, zs, rows, cols)
    got = exchange(payload)
    partial = jnp.sum(along_x.astype(F32), axis=0).astype(BF16)
    along_z = exchange(partial, z_groups)

    coadded, scaled = pl.pallas_call(
        coadd_kernel,
        out_shape=(SDS((rows, cols), F32), SDS((band, rows, cols), F32)),
        in_specs=[VM, VM, SM],
        out_specs=(VM, VM),
        name="coadd",
    )(along_z, got, gains)
    bands = exchange(scaled, None, "band")
    detection, measured = pl.pallas_call(
        measure_kernel,
        out_shape=(SDS((rows, cols), F32), SDS((sky, 2), F32)),
        in_specs=[VM, VM],
        out_specs=(VM, VM),
        name="measured",
    )(bands, got)
    returned = exchange(measured)
    fluxes = pl.pallas_call(
        pick_kernel,
        out_shape=SDS((1, profiles.shape[1]), F32),
        in_specs=[VM, VM],
        out_specs=VM,
        name="pick",
    )(returned, source_patch[:, :, 0])
    return coadded[None], detection, fluxes


def solution(mesh):
    return jax.shard_map(
        per_device,
        mesh=mesh,
        in_specs=(
            P("band", "sky", None, None),
            P("band", "sky", None),
            P("band", "sky", None),
            P("band", "sky"),
            P("band", "sky"),
            P("band", None),
            P("band", None, None),
            P("band", None, None),
            P("band"),
            P("band", "sky", None),
            P("band", "sky", None),
            P("band", "sky"),
        ),
        out_specs=(P("band", "sky", None), P("sky", None), P("band", "sky")),
        check_vma=False,
    )
```

time: 320 us -> 171 us (0.53)
  waiting for transfers between devices: 189 us -> 42.8 us
  blocking collectives: 32.5 us -> 72.4 us
  local copies, waits for them, and re-layouts: 30.9 us -> 1.79 us
  Pallas kernels: 0 us -> 21.1 us
  matrix products: 17.4 us -> 0 us
  starting transfers between devices: 38.5 us -> 29.3 us
  other arithmetic: 9.59 us -> 1.32 us
    all_to_all x3 -> x2, waiting for transfers between devices: 189 us -> 41.5 us  [exchange(): lax.all_to_all(value, axis, split_axis=0, concat_axis=0, tiled=True, axis...]
    all_to_all x1 -> x3, blocking collectives: 32.5 us -> 72.4 us  [exchange(): lax.all_to_all(value, axis, split_axis=0, concat_axis=0, tiled=True, axis...]
    pallas_call x0 -> x6, Pallas kernels: none -> 21.1 us  [the longest x1 7.08 us: per_device(): pl.pallas_call(match_kernel, out_shape=SDS((n, th, cols), BF16), in_specs...]
    all_to_all x3 -> x2, starting transfers between devices: 38.5 us -> 18.7 us  [exchange(): lax.all_to_all(value, axis, split_axis=0, concat_axis=0, tiled=True, axis...]
    dot_general x11 -> x0, matrix products: 17.4 us -> none  [the longest x2 4.71 us: match_tiles(): jnp.einsum('kia,nkal->nil', vertical, across, preferred_element_type=jnp....]
    all_to_all x5 -> x0, local copies, waits for them, and re-layouts: 16.1 us -> none  [the longest x2 15.3 us: in_one_piece(): lax.all_to_all(both, axis, split_axis=split_dim, concat_axis=concat_dim,...]
    slice x4 -> x0, local copies, waits for them, and re-layouts: 11.9 us -> none  [the longest x2 10.9 us: in_one_piece(): piece = out[..., at:at + column.shape[along]]]
    ppermute x0 -> x2, starting transfers between devices: none -> 10.7 us  [the longest x1 8.74 us: per_device(): other = lax.ppermute(matched, 'sky', partners)]
  transfers between devices with their start and end apart: 3 -> 4, of which waited for: 2 -> 3; matrix products, arithmetic and copies ran while one was open for 6% -> 1% of each run, Pallas kernels for 0% -> 1%
where the time goes in v1:
time: 171 us; the launch traced here: 170 us
  blocking collectives  72.4 us (42%)
  waiting for transfers between devices  42.8 us (25%)
  starting transfers between devices  29.3 us (17%)
  Pallas kernels  21.1 us (12%)
  local copies, waits for them, and re-layouts  1.79 us (1%)
    all_to_all x3, blocking collectives, exchange(): lax.all_to_all(value, axis, split_axis=0, concat_axis=0, tiled=True, axis...  72.4 us
    all_to_all x2, waiting for transfers between devices, exchange(): lax.all_to_all(value, axis, split_axis=0, concat_axis=0, tiled=True, axis...  41.5 us
    all_to_all x2, starting transfers between devices, exchange(): lax.all_to_all(value, axis, split_axis=0, concat_axis=0, tiled=True, axis...  18.7 us
    ppermute x1, starting transfers between devices, per_device(): other = lax.ppermute(matched, 'sky', partners)  8.74 us
    pallas_call x1, Pallas kernels, per_device(): pl.pallas_call(match_kernel, out_shape=SDS((n, th, cols), BF16), in_specs...  7.08 us
    pallas_call x1, Pallas kernels, per_device(): pl.pallas_call(place_kernel, out_shape=SDS((sky // 2, rows, cols), BF16),...  5.84 us
  transfers between devices with their start and end apart: 4, of which 3 were waited for; matrix products, arithmetic and copies ran while one was open for 1% of the time, Pallas kernels for 1%

profile of v1, /device:TPU:1, one launch (start us, length us, event | category | flops | bytes accessed | tf_op | source)
XLA Modules:
  0.0 170.0 jit_solution(188507508946065539)
XLA Ops:
  0.6 7.1 %match.1.m_ref = bf16[64,32,256]{2,1,0:T(8,128)(2,1)} custom-call(bf16[2048,256]{1,0:T(8,128)(2,1)} %bitcast.17, bf16[5,64]{1,0:T(8,128)(2,1)} %bitcast.21, bf16[5,41]{1,0:T(8,128)(2,1)} %bitcast.22, bf16[5,41]{1,0:T(8,128)(2,1)} %bitcast.23), custom_call_target="tpu_custom_call" | custom-call | tf_op jit(solution)/shard_map/match/pallas_call | solution.py:223
  7.7 8.7 %collective-permute-start.1 = (bf16[64,32,256]{2,1,0:T(8,128)(2,1)}, bf16[64,32,256]{2,1,0:T(8,128)(2,1)S(1)}, u32[]{:S(2)}, u32[]{:S(2)}) collective-permute-start(bf16[64,32,256]{2,1,0:T(8,128)(2,1)} %match.1.m_ref), channel_id=1, source_target_pairs={{0,4},{4,0},{8,12},{12,8},{16,20},{20,16},{24,28},{28,24},{32,36},... | collective-permute-start | bytes 3145736 | tf_op jit(solution)/shard_map/ppermute | solution.py:237
  16.5 2.1 %payload.1 = (s32[3,64]{1,0:T(4,128)}, bf16[128,8,128]{2,1,0:T(8,128)(2,1)}) custom-call(s32[1,64]{1,0:T(1,128)} %bitcast.26, s32[1,64]{1,0:T(1,128)} %to_ref.1, s32[1,64]{1,0:T(1,128)} %wi_ref.1, bf16[1,16]{1,0:T(2,128)(2,1)} %wt_ref.1, bf16[64,256]{1,0:T(8,128)(2,1)} %bitcast.20, s32[1,64]{1,0:T(1,128)} %bitcast.24, s32[1,64]{1,0:T(1,128)} %sr_ref.1), custom_call_target="tpu_custom_call" | custom-call | tf_op jit(solution)/shard_map/payload/pallas_call | solution.py:210
  18.5 1.9 %collective-permute-start = (s32[3,64]{1,0:T(4,128)}, s32[3,64]{1,0:T(4,128)S(1)}, u32[]{:S(2)}, u32[]{:S(2)}) collective-permute-start(s32[3,64]{1,0:T(4,128)} %get-tuple-element.9.mine_ref), channel_id=1, source_target_pairs={{0,4},{4,0},{8,12},{12,8},{16,20},{20,16},{24,28},{28,24},{32,36},... | collective-permute-start | bytes 2312 | tf_op jit(solution)/shard_map/ppermute | solution.py:221
  20.4 1.3 collective-permute-done.other_ref
  21.8 0.0 copy-start.3
  21.8 0.0 collective-permute-done.1.o_ref
  21.8 0.0 copy-start.2
  21.8 0.6 copy-done.3
  22.3 0.4 copy-done.2
  22.8 5.8 %place.1 = bf16[64,64,256]{2,1,0:T(8,128)(2,1)} custom-call(s32[1]{0:T(128)} %bitcast.core_ref, s32[3,64]{1,0:T(4,128)} %get-tuple-element.9.mine_ref, s32[3,64]{1,0:T(4,128)} %copy-done.3, bf16[64,32,256]{2,1,0:T(8,128)(2,1)} %match.1.m_ref, bf16[64,32,256]{2,1,0:T(8,128)(2,1)} %copy-done.2), custom_call_target="tpu_custom_call" | custom-call | tf_op jit(solution)/shard_map/place/pallas_call | solution.py:239
  28.6 29.7 %all_to_all.31 = bf16[64,64,256]{2,1,0:T(8,128)(2,1)S(1)} all-to-all(bf16[64,64,256]{2,1,0:T(8,128)(2,1)} %place.1), channel_id=1, replica_groups={{0,8,16,24},{4,12,20,28},{32,40,48,56},{36,44,52,60},{64,72,80,88},{68,..., dimensions={0} | all-to-all | bytes 4194304 | tf_op jit(solution)/shard_map/all_to_all | solution.py:192
  58.3 13.2 %all-to-all-start.2 = ((bf16[128,8,128]{2,1,0:T(8,128)(2,1)}), bf16[128,8,128]{2,1,0:T(8,128)(2,1)S(1)}, u32[]{:S(2)}, u32[]{:S(2)}) async-start(bf16[128,8,128]{2,1,0:T(8,128)(2,1)} %get-tuple-element.10), calls=%async_computation.2 | async-start | bytes 524288 | tf_op jit(solution)/shard_map/all_to_all | solution.py:192
  71.5 1.3 reduce_sum.12
  72.8 19.1 %all-to-all-done.2.got_ref = bf16[128,8,128]{2,1,0:T(8,128)(2,1)S(1)} async-done(((bf16[128,8,128]{2,1,0:T(8,128)(2,1)}), bf16[128,8,128]{2,1,0:T(8,128)(2,1)S(1)}, u32[]{:S(2)}, u32[]{:S(2)}) %all-to-all-start.2) | async-done | bytes 262176 | tf_op jit(solution)/shard_map/all_to_all | solution.py:192
  92.0 5.4 %all-to-all-start.1 = ((bf16[16,64,256]{2,1,0:T(8,128)(2,1)}), bf16[16,64,256]{2,1,0:T(8,128)(2,1)S(1)}, u32[]{:S(2)}, u32[]{:S(2)}) async-start(bf16[16,64,256]{2,1,0:T(8,128)(2,1)} %reduce_sum.12), calls=%async_computation.1 | async-start | bytes 1048576 | tf_op jit(solution)/shard_map/all_to_all | solution.py:192
  98.1 22.4 %all-to-all-done.1.parts_ref = bf16[16,64,256]{2,1,0:T(8,128)(2,1)S(1)} async-done(((bf16[16,64,256]{2,1,0:T(8,128)(2,1)}), bf16[16,64,256]{2,1,0:T(8,128)(2,1)S(1)}, u32[]{:S(2)}, u32[]{:S(2)}) %all-to-all-start.1) | async-done | bytes 524320 | tf_op jit(solution)/shard_map/all_to_all | solution.py:192
  120.5 0.0 copy-done
  120.5 0.8 copy-done.1
  121.2 2.3 %coadd.1 = (f32[64,256]{1,0:T(8,128)}, f32[4,64,256]{2,1,0:T(8,128)}) custom-call(bf16[16,64,256]{2,1,0:T(8,128)(2,1)} %copy-done.1, bf16[128,8,128]{2,1,0:T(8,128)(2,1)} %copy-done, f32[1]{0:T(128)S(6)} %copy.16.gain_ref), custom_call_target="tpu_custom_call" | custom-call | tf_op jit(solution)/shard_map/coadd/pallas_call | solution.py:253
  123.6 10.0 %all_to_all.32.bands_ref = f32[4,64,256]{2,1,0:T(8,128)} all-to-all(f32[4,64,256]{2,1,0:T(8,128)} %get-tuple-element.12), channel_id=1, replica_groups=mesh['sky'=128,'band'=4] {'band'}, dimensions={0} | all-to-all | bytes 524288 | tf_op jit(solution)/shard_map/all_to_all | solution.py:192
  133.5 2.3 %measured.1 = (f32[64,256]{1,0:T(8,128)}, f32[128,2]{1,0:T(8,128)}) custom-call(f32[4,64,256]{2,1,0:T(8,128)} %all_to_all.32.bands_ref, bf16[128,8,128]{2,1,0:T(8,128)(2,1)} %copy-done), custom_call_target="tpu_custom_call" | custom-call | tf_op jit(solution)/shard_map/measured/pallas_call | solution.py:261
  135.8 32.7 %all_to_all.33 = f32[128,1,2]{2,1,0:T(1,128)} all-to-all(f32[128,1,2]{2,1,0:T(1,128)} %bitcast.19), channel_id=1, replica_groups=mesh['sky'=128,'band'=4] {'sky'}, dimensions={0} | all-to-all | bytes 2048 | tf_op jit(solution)/shard_map/all_to_all | solution.py:192
  168.5 1.5 pick.1
  (2 shorter events, 0.0 us)
Async XLA Ops:
  7.7 14.1 %collective-permute-start.1 = (bf16[64,32,256]{2,1,0:T(8,128)(2,1)}, bf16[64,32,256]{2,1,0:T(8,128)(2,1)S(1)}, u32[]{:S(2)}, u32[]{:S(2)}) collective-permute-start(bf16[64,32,256]{2,1,0:T(8,128)(2,1)} %match.1.m_ref), channel_id=1, source_target_pairs={{0,4},{4,0},{8,12},{12,8},{16,20},{20,16},{24,28},{28,24},{32,36},... | collective-permute-start | bytes 3145736 | tf_op jit(solution)/shard_map/ppermute | solution.py:237
  18.5 3.3 %collective-permute-start = (s32[3,64]{1,0:T(4,128)}, s32[3,64]{1,0:T(4,128)S(1)}, u32[]{:S(2)}, u32[]{:S(2)}) collective-permute-start(s32[3,64]{1,0:T(4,128)} %get-tuple-element.9.mine_ref), channel_id=1, source_target_pairs={{0,4},{4,0},{8,12},{12,8},{16,20},{20,16},{24,28},{28,24},{32,36},... | collective-permute-start | bytes 2312 | tf_op jit(solution)/shard_map/ppermute | solution.py:221
  21.8 0.6 copy-start.3
  21.8 1.0 copy-start.2
  58.3 33.7 %all-to-all-start.2 = ((bf16[128,8,128]{2,1,0:T(8,128)(2,1)}), bf16[128,8,128]{2,1,0:T(8,128)(2,1)S(1)}, u32[]{:S(2)}, u32[]{:S(2)}) async-start(bf16[128,8,128]{2,1,0:T(8,128)(2,1)} %get-tuple-element.10), calls=%async_computation.2 | async-start | bytes 524288 | tf_op jit(solution)/shard_map/all_to_all | solution.py:192
  92.0 28.5 %copy-start = (bf16[128,8,128]{2,1,0:T(8,128)(2,1)}, bf16[128,8,128]{2,1,0:T(8,128)(2,1)S(1)}, u32[]{:S(2)}) copy-start(bf16[128,8,128]{2,1,0:T(8,128)(2,1)S(1)} %all-to-all-done.2.got_ref) | copy-start | bytes 786436
  92.0 28.5 %all-to-all-start.1 = ((bf16[16,64,256]{2,1,0:T(8,128)(2,1)}), bf16[16,64,256]{2,1,0:T(8,128)(2,1)S(1)}, u32[]{:S(2)}, u32[]{:S(2)}) async-start(bf16[16,64,256]{2,1,0:T(8,128)(2,1)} %reduce_sum.12), calls=%async_computation.1 | async-start | bytes 1048576 | tf_op jit(solution)/shard_map/all_to_all | solution.py:192
  120.5 0.8 copy-start.1

commit v2 on v1

v2 whole, which is shorter than its diff:
```python
import jax
import jax.numpy as jnp
from jax import lax
from jax.experimental import pallas as pl
from jax.experimental.pallas import tpu as pltpu
from jax.sharding import PartitionSpec as P

F32 = jnp.float32
BF16 = jnp.bfloat16
I32 = jnp.int32
NT = (((1,), (1,)), ((), ()))
TN = (((0,), (0,)), ((), ()))


def iota(shape, dim):
    return lax.broadcasted_iota(I32, shape, dim)


def as_column(row):
    n = row.shape[1]
    eye = iota((n, n), 0) == iota((n, n), 1)
    return jnp.sum(jnp.where(eye, jnp.broadcast_to(row, (n, n)), jnp.zeros_like(row)), axis=1, keepdims=True)


def ranks(patch):
    n = patch.shape[1]
    column = as_column(patch)
    same = (column == patch) & (iota((n, n), 0) < iota((n, n), 1))
    return jnp.sum(same.astype(I32), axis=0, keepdims=True)


def write_details(out_ref, tp_ref, to_ref, wi_ref, wt_ref, sp_ref, sr_ref):
    n = tp_ref.shape[1]
    visits = wt_ref.shape[1]
    table = as_column(wt_ref[...].astype(F32))
    weight = jnp.sum(jnp.where(iota((visits, n), 0) == wi_ref[...], table, 0.0), axis=0, keepdims=True)
    rows = [tp_ref[...].astype(F32), to_ref[...].astype(F32), weight]
    rows += [sp_ref[...].astype(F32), sr_ref[...].astype(F32), ranks(sp_ref[...]).astype(F32)]
    rows.append(jnp.zeros((8 - len(rows), n), F32))
    block = jnp.concatenate(rows, axis=0).astype(BF16)
    out_ref[out_ref.shape[0] - 1, 0:8, 0:128] = jnp.concatenate([block, jnp.zeros((8, 128 - n), BF16)], axis=1)


def match_kernel(
    tiles_ref, coef_ref, tr_ref, tc_ref, tp_ref, to_ref, wi_ref, wt_ref, sp_ref, sr_ref,
    out_ref, taps_s, v_s, u_s, ce_s, a_s,
):
    write_details(out_ref, tp_ref, to_ref, wi_ref, wt_ref, sp_ref, sr_ref)
    basis, tap_total = tc_ref.shape
    half = (tap_total - 1) // 2
    cols = tiles_ref.shape[1]
    th = out_ref.shape[1]
    group = 256 // th
    taps_s[...] = jnp.zeros(taps_s.shape, F32)
    taps_s[0:basis, 0:tap_total] = tc_ref[...].astype(F32)
    taps_s[8 : 8 + basis, 0:tap_total] = tr_ref[...].astype(F32)
    taps_s[...] = pltpu.roll(taps_s[...], cols - half, 1)
    lag = iota((cols, cols), 1) - iota((cols, cols), 0)
    inside = (lag >= -half) & (lag <= half)
    for k in range(basis):
        rows = jnp.broadcast_to(taps_s[k : k + 1, :], (cols, cols))
        rolled = pltpu.roll(rows, 0, 1, stride=1, stride_axis=0)
        v_s[k] = jnp.where(inside, rolled, 0.0).astype(BF16)
    parts = []
    for k in range(basis):
        rows = jnp.broadcast_to(taps_s[8 + k : 9 + k, :], (th, cols))
        rolled = pltpu.roll(rows, 0, 1, stride=1, stride_axis=0)
        parts.append(jnp.where(inside[0:th, :], rolled, 0.0)[:, 0:128])
    parts.append(jnp.zeros((256 - basis * th, 128), F32))
    vertical = jnp.concatenate(parts, axis=0).T
    u_s[...] = vertical[0:th, 0 : basis * th].astype(BF16)
    n = coef_ref.shape[1]
    spread = (iota((n * th, n), 0) // th == iota((n * th, n), 1)).astype(F32).astype(BF16)
    ce_s[:, 0:basis] = lax.dot_general(spread, coef_ref[...], NT, preferred_element_type=F32)

    def one_group(g, carry):
        start = pl.multiple_of(g * 256, 256)
        pixels = tiles_ref[pl.ds(start, 256), :]
        coef = ce_s[pl.ds(start, 256), :]
        for k in range(basis):
            across = jnp.dot(pixels, v_s[k], preferred_element_type=F32)
            across = (across * coef[:, k : k + 1]).astype(BF16)
            a_s[:, k * th : (k + 1) * th, :] = across.reshape(group, th, cols)
        for t in range(group):
            done = jnp.dot(u_s[...], a_s[t], preferred_element_type=F32)
            out_ref[g * group + t] = done.astype(BF16)
        return carry

    lax.fori_loop(0, n // group, one_group, 0)


def place_kernel(here_ref, m_ref, o_ref, out_ref, canvas, words_s, words, sem):
    core = here_ref[0]
    first = here_ref[1]
    n = m_ref.shape[0] - 1
    th = m_ref.shape[1]
    rows = 2 * th
    for i, strips in enumerate((m_ref, o_ref)):
        details = strips[n, 0:8, 0:128].astype(F32)
        scale = jnp.where(iota(details.shape, 0) == 2, 256.0, 1.0)
        words_s[i] = (details * scale).astype(I32)
    copy = pltpu.make_async_copy(words_s, words, sem)
    copy.start()
    canvas[...] = jnp.zeros(canvas.shape, F32)
    copy.wait()
    depth = canvas.shape[0] // 8
    lane = iota((1, 128), 1)

    def place_of(patch):
        q = patch >> 1
        x, z = q & 3, q >> 2
        return ((z & 1) * 4 + x) * depth + (z >> 1)

    for i, strips in enumerate((m_ref, o_ref)):
        slots = first + 2 * (core if i == 0 else 1 - core)

        def one(t, carry, i=i, strips=strips, slots=slots):
            patch = words[i, 0, t]

            @pl.when((patch & 1) == core)
            def _():
                at = place_of(patch)
                off = words[i, 1, t]
                w = words[i, 2, t].astype(F32) * (1.0 / 256.0)
                strip = strips[t].astype(F32) * w
                for h in range(canvas.shape[1]):
                    canvas[at, h, pl.ds(off, th), :] += strip[:, h * 128 : (h + 1) * 128]
                covered = (lane >= off) & (lane < off + th)
                canvas[at, 0, rows : rows + 1, :] += jnp.where(covered, w, 0.0)

            patch_s = words[i, 3, t]

            @pl.when((patch_s & 1) == core)
            def _():
                at = place_of(patch_s)
                slot = slots + words[i, 5, t]
                value = words[i, 4, t].astype(F32)
                for h in range(canvas.shape[1]):
                    canvas[at, h, rows + 1 : rows + 2, :] += jnp.where(lane == slot - h * 128, value, 0.0)

            return carry

        lax.fori_loop(0, n, one, 0)
    for h in range(canvas.shape[1]):
        out_ref[:, :, h * 128 : (h + 1) * 128] = canvas[:, h].astype(BF16)


def add_kernel(parts_ref, out_ref):
    out_ref[...] = jnp.sum(parts_ref[...].astype(F32), axis=0).astype(BF16)


def coadd_kernel(parts_ref, gain_ref, out_ref, scaled_ref, asked_ref):
    rows, cols = out_ref.shape
    summed = jnp.sum(parts_ref[...].astype(F32), axis=0)
    column = as_column(jnp.maximum(summed[rows : rows + 1, 0:rows], 1.0))
    coadded = summed[0:rows] / column
    out_ref[...] = coadded
    scaled_ref[...] = jnp.broadcast_to((gain_ref[0] * coadded)[None], scaled_ref.shape)
    asked_ref[...] = summed[rows + 1 : rows + 2]


def detect_kernel(bands_ref, asked_ref, det_ref, rows_ref):
    detection = jnp.sum(bands_ref[...], axis=0)
    det_ref[...] = detection
    rows = det_ref.shape[0]
    ids = iota((rows, asked_ref.shape[1]), 0).astype(F32)
    hot = (ids == asked_ref[...]).astype(F32).astype(BF16)
    picked = lax.dot_general(hot, detection.astype(BF16), TN, preferred_element_type=F32)
    rows_ref[...] = picked.astype(BF16)


def flux_kernel(rows_ref, prof_ref, sp_ref, out_ref):
    patch = sp_ref[...]
    slot = 2 * patch + ranks(patch)
    each = lax.dot_general(rows_ref[...], prof_ref[...], NT, preferred_element_type=F32)
    wanted = iota(each.shape, 0) == slot
    out_ref[...] = jnp.sum(jnp.where(wanted, each, 0.0), axis=0, keepdims=True)


VM = pl.BlockSpec(memory_space=pltpu.VMEM)
SM = pl.BlockSpec(memory_space=pltpu.SMEM)
SDS = jax.ShapeDtypeStruct


def grant(mib):
    return pltpu.CompilerParams(vmem_limit_bytes=mib << 20)


def exchange(value, groups=None, axis="sky"):
    return lax.all_to_all(value, axis, split_axis=0, concat_axis=0, tiled=True, axis_index_groups=groups)


def per_device(
    tiles, coefs, tile_patch, tile_offset, weight_index, weight_table,
    taps_rows, taps_cols, gains, profiles, source_patch, source_row,
):
    sky = lax.axis_size("sky")
    band = lax.axis_size("band")
    _, n, th, cols = tiles.shape
    rows = 2 * th
    high = rows + 8
    basis = coefs.shape[2]
    depth = sky // 16
    sky_of = lambda z, x, c: (z * 4 + x) * 2 + c
    near = [[sky_of(2 * m + b, x, c) for b in range(2) for x in range(4)] for m in range(depth) for c in range(2)]
    far = [[sky_of(2 * m + b, x, c) for m in range(depth)] for b in range(2) for x in range(4) for c in range(2)]
    partners = [(i, i ^ 1) for i in range(sky)]
    me = lax.axis_index("sky").astype(I32)
    here = jnp.stack([me & 1, 2 * (me & ~1)])

    matched = pl.pallas_call(
        match_kernel,
        out_shape=SDS((n + 1, th, cols), BF16),
        in_specs=[VM] * 10,
        out_specs=VM,
        scratch_shapes=[
            pltpu.VMEM((16, cols), F32),
            pltpu.VMEM((basis, cols, cols), BF16),
            pltpu.VMEM((th, basis * th), BF16),
            pltpu.VMEM((n * th, 8), F32),
            pltpu.VMEM((256 // th, basis * th, cols), BF16),
        ],
        name="match",
        compiler_params=grant(10),
    )(
        tiles.reshape(n * th, cols), coefs[0].T, taps_rows[0], taps_cols[0],
        tile_patch[:, :, 0], tile_offset, weight_index, weight_table, source_patch[:, :, 0], source_row,
    )
    other = lax.ppermute(matched, "sky", partners)

    canvas = pl.pallas_call(
        place_kernel,
        out_shape=SDS((sky // 2, high, cols), BF16),
        in_specs=[SM, VM, VM],
        out_specs=VM,
        scratch_shapes=[
            pltpu.VMEM((sky // 2, cols // 128, high, 128), F32),
            pltpu.VMEM((2, 8, 128), I32),
            pltpu.SMEM((2, 8, 128), I32),
            pltpu.SemaphoreType.DMA,
        ],
        name="place",
        compiler_params=grant(14),
    )(here, matched, other)

    along_x = exchange(canvas, near).reshape(8, depth, high, cols)
    partial = pl.pallas_call(
        add_kernel, out_shape=SDS((depth, high, cols), BF16), in_specs=[VM], out_specs=VM, name="add",
        compiler_params=grant(8),
    )(along_x)
    along_z = exchange(partial, far)

    coadded, scaled, asked = pl.pallas_call(
        coadd_kernel,
        out_shape=(SDS((rows, cols), F32), SDS((band, rows, cols), F32), SDS((1, cols), F32)),
        in_specs=[VM, SM],
        out_specs=(VM, VM, VM),
        name="coadd",
        compiler_params=grant(4),
    )(along_z, gains)
    bands = exchange(scaled, None, "band")
    detection, picked = pl.pallas_call(
        detect_kernel,
        out_shape=(SDS((rows, cols), F32), SDS((2 * sky, cols), BF16)),
        in_specs=[VM, VM],
        out_specs=(VM, VM),
        name="detect",
        compiler_params=grant(4),
    )(bands, asked)
    returned = exchange(picked.reshape(sky, 2, cols)).reshape(2 * sky, cols)
    fluxes = pl.pallas_call(
        flux_kernel,
        out_shape=SDS((1, profiles.shape[1]), F32),
        in_specs=[VM, VM, VM],
        out_specs=VM,
        name="flux",
        compiler_params=grant(4),
    )(returned, profiles[0], source_patch[:, :, 0])
    return coadded[None], detection, fluxes


def solution(mesh):
    return jax.shard_map(
        per_device,
        mesh=mesh,
        in_specs=(
            P("band", "sky", None, None),
            P("band", "sky", None),
            P("band", "sky", None),
            P("band", "sky"),
            P("band", "sky"),
            P("band", None),
            P("band", None, None),
            P("band", None, None),
            P("band"),
            P("band", "sky", None),
            P("band", "sky", None),
            P("band", "sky"),
        ),
        out_specs=(P("band", "sky", None), P("sky", None), P("band", "sky")),
        check_vma=False,
    )
```

time: 171 us -> 132 us (0.77)
  waiting for transfers between devices: 42.8 us -> 20.9 us
  starting transfers between devices: 29.3 us -> 20.2 us
  Pallas kernels: 21.1 us -> 14.2 us
  local copies, waits for them, and re-layouts: 1.79 us -> 7.31 us
  blocking collectives: 72.4 us -> 67.5 us
    all_to_all x2 -> x1, waiting for transfers between devices: 41.5 us -> 18.7 us  [exchange(): lax.all_to_all(value, axis, split_axis=0, concat_axis=0, tiled=True, axis...]
    all_to_all x2 -> x1, starting transfers between devices: 18.7 us -> 11.5 us  [exchange(): lax.all_to_all(value, axis, split_axis=0, concat_axis=0, tiled=True, axis...]
    unnamed x8 -> x24, local copies, waits for them, and re-layouts: 1.79 us -> 7.2 us
    pallas_call x5, Pallas kernels: 18.7 us -> 13.4 us  [the longest x1 6.2 us: per_device(): pl.pallas_call(place_kernel, out_shape=SDS((sky // 2, high, cols), BF16),...]
    all_to_all x3, blocking collectives: 72.4 us -> 67.5 us  [exchange(): lax.all_to_all(value, axis, split_axis=0, concat_axis=0, tiled=True, axis...]
    ppermute x1, waiting for transfers between devices: 0.01 us -> 2.21 us  [per_device(): other = lax.ppermute(matched, 'sky', partners)]
    ppermute x1 -> x0, starting transfers between devices: 1.91 us -> none  [per_device(): other_meta = lax.ppermute(meta, 'sky', partners)]
  transfers between devices with their start and end apart: 4 -> 2, of which waited for: 3 -> 2; matrix products, arithmetic and copies ran while one was open for 1% -> 0% of each run, Pallas kernels for 1% -> 0%
where the time goes in v2:
time: 132 us
  blocking collectives  67.5 us (51%)
  waiting for transfers between devices  20.9 us (16%)
  starting transfers between devices  20.2 us (15%)
  Pallas kernels  14.2 us (11%)
  local copies, waits for them, and re-layouts  7.31 us (6%)
  between operations  1.35 us (1%)
    all_to_all x3, blocking collectives, exchange(): lax.all_to_all(value, axis, split_axis=0, concat_axis=0, tiled=True, axis...  67.5 us
    all_to_all x1, waiting for transfers between devices, exchange(): lax.all_to_all(value, axis, split_axis=0, concat_axis=0, tiled=True, axis...  18.7 us
    all_to_all x1, starting transfers between devices, exchange(): lax.all_to_all(value, axis, split_axis=0, concat_axis=0, tiled=True, axis...  11.5 us
    ppermute x1, starting transfers between devices, per_device(): other = lax.ppermute(matched, 'sky', partners)  8.74 us
    unnamed x24, local copies, waits for them, and re-layouts  7.2 us
    pallas_call x1, Pallas kernels, per_device(): pl.pallas_call(place_kernel, out_shape=SDS((sky // 2, high, cols), BF16),...  6.2 us
    pallas_call x1, Pallas kernels, per_device(): pl.pallas_call(match_kernel, out_shape=SDS((n + 1, th, cols), BF16), in_s...  4.86 us
  transfers between devices with their start and end apart: 2, of which 2 were waited for; matrix products, arithmetic and copies ran while one was open for 0% of the time, Pallas kernels for 0%

profile of v2, /device:TPU:1, one launch (start us, length us, event | category | flops | bytes accessed | tf_op | source)
XLA Modules:
  0.0 131.5 jit_solution(10263653788737344104)
XLA Ops:
  0.6 1.2 copy-done
  1.9 0.7 copy-done.2
  2.5 0.7 copy-done.3
  3.2 0.7 copy-done.4
  3.9 0.7 copy-done.5
  4.6 0.7 copy-done.7
  5.2 0.7 copy-done.8
  5.9 0.7 copy-done.9
  6.5 0.7 copy-done.10
  7.2 0.7 copy-done.11
  7.8 4.9 %match.1.m_ref = bf16[65,32,256]{2,1,0:T(8,128)(2,1)S(1)} custom-call(bf16[2048,256]{1,0:T(8,128)(2,1)S(1)} %bitcast.14, bf16[5,64]{1,0:T(8,128)(2,1)S(1)} %bitcast.16, bf16[5,41]{1,0:T(8,128)(2,1)S(1)} %bitcast.17, bf16[5,41]{1,0:T(8,128)(2,1)S(1)} %bitcast.18, s32[1,64]{1,0:T(1,128)S(1)} %bitcast.21, s32[1,64]{1,0:T(1,128)S(1)} %copy-done.8, ...), custom_call_target="tpu_custom_call" | custom-call | tf_op jit(solution)/shard_map/match/pallas_call | solution.py:211
  12.7 8.7 %collective-permute-start = (bf16[65,32,256]{2,1,0:T(8,128)(2,1)S(1)}, bf16[65,32,256]{2,1,0:T(8,128)(2,1)S(1)}, u32[]{:S(2)}, u32[]{:S(2)}) collective-permute-start(bf16[65,32,256]{2,1,0:T(8,128)(2,1)S(1)} %match.1.m_ref), channel_id=1, source_target_pairs={{0,4},{4,0},{8,12},{12,8},{16,20},{20,16},{24,28},{28,24},{32,36},... | collective-permute-start | bytes 3194888 | tf_op jit(solution)/shard_map/ppermute | solution.py:229
  21.5 0.1 pad_add_fusion.here_ref
  21.5 2.2 %collective-permute-done.o_ref = bf16[65,32,256]{2,1,0:T(8,128)(2,1)S(1)} collective-permute-done((bf16[65,32,256]{2,1,0:T(8,128)(2,1)S(1)}, bf16[65,32,256]{2,1,0:T(8,128)(2,1)S(1)}, u32[]{:S(2)}, u32[]{:S(2)}) %collective-permute-start) | collective-permute-done | bytes 1064992 | tf_op jit(solution)/shard_map/ppermute | solution.py:229
  23.7 6.2 %place.1 = bf16[64,72,256]{2,1,0:T(8,128)(2,1)S(1)} custom-call(s32[2]{0:T(128)S(1)} %pad_add_fusion.here_ref, bf16[65,32,256]{2,1,0:T(8,128)(2,1)S(1)} %match.1.m_ref, bf16[65,32,256]{2,1,0:T(8,128)(2,1)S(1)} %collective-permute-done.o_ref), custom_call_target="tpu_custom_call" | custom-call | tf_op jit(solution)/shard_map/place/pallas_call | solution.py:231
  29.9 30.9 %all_to_all.20 = bf16[64,72,256]{2,1,0:T(8,128)(2,1)S(1)} all-to-all(bf16[64,72,256]{2,1,0:T(8,128)(2,1)S(1)} %place.1), channel_id=1, replica_groups={{0,8,16,24,32,40,48,56},{4,12,20,28,36,44,52,60},{64,72,80,88,96,104,11..., dimensions={0} | all-to-all | bytes 4718592 | tf_op jit(solution)/shard_map/all_to_all | solution.py:190
  60.8 1.0 add.3
  61.8 11.5 %all-to-all-start.1 = ((bf16[8,72,256]{2,1,0:T(8,128)(2,1)}), bf16[8,72,256]{2,1,0:T(8,128)(2,1)S(1)}, u32[]{:S(2)}, u32[]{:S(2)}) async-start(bf16[8,72,256]{2,1,0:T(8,128)(2,1)} %add.3), calls=%async_computation.1 | async-start | bytes 589824 | tf_op jit(solution)/shard_map/all_to_all | solution.py:190
  73.9 18.7 %all-to-all-done.1.parts_ref = bf16[8,72,256]{2,1,0:T(8,128)(2,1)S(1)} async-done(((bf16[8,72,256]{2,1,0:T(8,128)(2,1)}), bf16[8,72,256]{2,1,0:T(8,128)(2,1)S(1)}, u32[]{:S(2)}, u32[]{:S(2)}) %all-to-all-start.1) | async-done | bytes 294944 | tf_op jit(solution)/shard_map/all_to_all | solution.py:190
  92.7 0.7 coadd.1
  93.4 8.6 %all_to_all.21.bands_ref = f32[4,64,256]{2,1,0:T(8,128)S(1)} all-to-all(f32[4,64,256]{2,1,0:T(8,128)S(1)} %get-tuple-element.9), channel_id=1, replica_groups=mesh['sky'=128,'band'=4] {'band'}, dimensions={0} | all-to-all | bytes 524288 | tf_op jit(solution)/shard_map/all_to_all | solution.py:190
  102.0 0.7 detect.1
  102.7 28.0 %all_to_all.22 = bf16[128,2,256]{2,1,0:T(2,128)(2,1)S(1)} all-to-all(bf16[128,2,256]{2,1,0:T(2,128)(2,1)S(1)} %reshape.20), channel_id=1, replica_groups=mesh['sky'=128,'band'=4] {'sky'}, dimensions={0} | all-to-all | bytes 262144 | tf_op jit(solution)/shard_map/all_to_all | solution.py:190
  130.8 0.7 flux.1
  (16 shorter events, 0.1 us)
Async XLA Ops:
  0.6 1.2 copy-start
  1.9 0.7 copy-start.2
  2.5 0.7 copy-start.3
  3.2 0.7 copy-start.4
  3.9 0.7 copy-start.5
  4.6 0.7 copy-start.7
  5.2 0.7 copy-start.8
  5.9 0.7 copy-start.9
  6.5 0.7 copy-start.10
  7.2 0.7 copy-start.11
  12.7 11.0 %collective-permute-start = (bf16[65,32,256]{2,1,0:T(8,128)(2,1)S(1)}, bf16[65,32,256]{2,1,0:T(8,128)(2,1)S(1)}, u32[]{:S(2)}, u32[]{:S(2)}) collective-permute-start(bf16[65,32,256]{2,1,0:T(8,128)(2,1)S(1)} %match.1.m_ref), channel_id=1, source_target_pairs={{0,4},{4,0},{8,12},{12,8},{16,20},{20,16},{24,28},{28,24},{32,36},... | collective-permute-start | bytes 3194888 | tf_op jit(solution)/shard_map/ppermute | solution.py:229
  60.8 70.0 %copy-start.1 = (bf16[1,64,256]{2,1,0:T(8,128)(2,1)S(1)}, bf16[1,64,256]{2,1,0:T(8,128)(2,1)}, u32[]{:S(2)}) copy-start(bf16[1,64,256]{2,1,0:T(8,128)(2,1)} %param.21) | copy-start | bytes 98308
  60.8 70.0 %copy-start.6 = (s32[1,64,1]{1,2,0:T(1,128)S(1)}, s32[1,64,1]{1,2,0:T(1,128)}, u32[]{:S(2)}) copy-start(s32[1,64,1]{1,2,0:T(1,128)} %param.22) | copy-start | bytes 772
  61.8 30.8 %all-to-all-start.1 = ((bf16[8,72,256]{2,1,0:T(8,128)(2,1)}), bf16[8,72,256]{2,1,0:T(8,128)(2,1)S(1)}, u32[]{:S(2)}, u32[]{:S(2)}) async-start(bf16[8,72,256]{2,1,0:T(8,128)(2,1)} %add.3), calls=%async_computation.1 | async-start | bytes 589824 | tf_op jit(solution)/shard_map/all_to_all | solution.py:190

commit v3 on v2

--- a/solution.py
+++ b/solution.py
@@ -41,8 +41,19 @@
     out_ref[out_ref.shape[0] - 1, 0:8, 0:128] = jnp.concatenate([block, jnp.zeros((8, 128 - n), BF16)], axis=1)
 
 
-def match_kernel(
-    tiles_ref, coef_ref, tr_ref, tc_ref, tp_ref, to_ref, wi_ref, wt_ref, sp_ref, sr_ref,
+def match_kernel(*refs):
+    sources, out_ref, scratch = refs[:10], refs[10], refs[11:]
+    inner, held, sems = scratch[:5], scratch[5:15], scratch[15]
+    copies = [pltpu.make_async_copy(src, dst, sems.at[i]) for i, (src, dst) in enumerate(zip(sources, held))]
+    for copy in copies[::-1]:
+        copy.start()
+    for copy in copies[1:]:
+        copy.wait()
+    match_body(copies[0], *held, out_ref, *inner)
+
+
+def match_body(
+    tiles_copy, tiles_ref, coef_ref, tr_ref, tc_ref, tp_ref, to_ref, wi_ref, wt_ref, sp_ref, sr_ref,
     out_ref, taps_s, v_s, u_s, ce_s, a_s,
 ):
     write_details(out_ref, tp_ref, to_ref, wi_ref, wt_ref, sp_ref, sr_ref)
@@ -73,6 +84,8 @@
     spread = (iota((n * th, n), 0) // th == iota((n * th, n), 1)).astype(F32).astype(BF16)
     ce_s[:, 0:basis] = lax.dot_general(spread, coef_ref[...], NT, preferred_element_type=F32)
 
+    tiles_copy.wait()
+
     def one_group(g, carry):
         start = pl.multiple_of(g * 256, 256)
         pixels = tiles_ref[pl.ds(start, 256), :]
@@ -89,60 +102,63 @@
     lax.fori_loop(0, n // group, one_group, 0)
 
 
-def place_kernel(here_ref, m_ref, o_ref, out_ref, canvas, words_s, words, sem):
-    core = here_ref[0]
-    first = here_ref[1]
+def place_kernel(me_ref, m_ref, o_ref, out_ref, canvas, words_s, words, sem):
+    core = me_ref[0] & 1
+    first = 2 * (me_ref[0] - core)
     n = m_ref.shape[0] - 1
     th = m_ref.shape[1]
     rows = 2 * th
-    for i, strips in enumerate((m_ref, o_ref)):
-        details = strips[n, 0:8, 0:128].astype(F32)
-        scale = jnp.where(iota(details.shape, 0) == 2, 256.0, 1.0)
-        words_s[i] = (details * scale).astype(I32)
-    copy = pltpu.make_async_copy(words_s, words, sem)
-    copy.start()
-    canvas[...] = jnp.zeros(canvas.shape, F32)
-    copy.wait()
-    depth = canvas.shape[0] // 8
-    lane = iota((1, 128), 1)
+    total = out_ref.shape[0]
+    depth = total // 4
 
     def place_of(patch):
         q = patch >> 1
         x, z = q & 3, q >> 2
-        return ((z & 1) * 4 + x) * depth + (z >> 1)
-
+        return jnp.where((patch & 1) == core, x * depth + z, total)
+
+    coverage = jnp.zeros((total, 128), F32)
+    requests = jnp.zeros((total, 256), F32)
+    lane = iota((n, 256), 1)
+    copies = []
     for i, strips in enumerate((m_ref, o_ref)):
-        slots = first + 2 * (core if i == 0 else 1 - core)
-
-        def one(t, carry, i=i, strips=strips, slots=slots):
-            patch = words[i, 0, t]
-
-            @pl.when((patch & 1) == core)
-            def _():
-                at = place_of(patch)
-                off = words[i, 1, t]
-                w = words[i, 2, t].astype(F32) * (1.0 / 256.0)
-                strip = strips[t].astype(F32) * w
-                for h in range(canvas.shape[1]):
-                    canvas[at, h, pl.ds(off, th), :] += strip[:, h * 128 : (h + 1) * 128]
-                covered = (lane >= off) & (lane < off + th)
-                canvas[at, 0, rows : rows + 1, :] += jnp.where(covered, w, 0.0)
-
-            patch_s = words[i, 3, t]
-
-            @pl.when((patch_s & 1) == core)
-            def _():
-                at = place_of(patch_s)
-                slot = slots + words[i, 5, t]
-                value = words[i, 4, t].astype(F32)
-                for h in range(canvas.shape[1]):
-                    canvas[at, h, rows + 1 : rows + 2, :] += jnp.where(lane == slot - h * 128, value, 0.0)
-
+        details = strips[n, 0:8, 0:128].astype(F32)[:, 0:n]
+        patch, offset, patch_s = (details[r : r + 1].astype(I32) for r in (0, 1, 3))
+        weight, row_s, rank_s = (details[r : r + 1] for r in (2, 4, 5))
+        at = place_of(patch)
+        words_s[i, 0:1, 0:n] = at
+        words_s[i, 1:2, 0:n] = offset
+        words_s[i, 2:3, 0:n] = (weight * 256.0).astype(I32)
+        copies.append(pltpu.make_async_copy(words_s.at[i], words.at[i], sem.at[i]))
+        copies[-1].start()
+        off_col = as_column(offset)
+        covered = (lane >= off_col) & (lane < off_col + th)
+        covers = jnp.where(covered, as_column(weight), 0.0)[:, 0:128].astype(BF16)
+        here = (iota((total, n), 0) == at).astype(F32).astype(BF16)
+        coverage += jnp.dot(here, covers, preferred_element_type=F32)
+        slot = rank_s.astype(I32) + (first + 2 * (core if i == 0 else 1 - core))
+        asks = jnp.where(lane == as_column(slot), as_column(row_s), 0.0).astype(BF16)
+        there = (iota((total, n), 0) == place_of(patch_s)).astype(F32).astype(BF16)
+        requests += jnp.dot(there, asks, preferred_element_type=F32)
+    canvas[...] = jnp.zeros(canvas.shape, F32)
+    canvas[0:total, 0, rows, :] = coverage
+    for h in range(canvas.shape[1]):
+        canvas[0:total, h, rows + 1, :] = requests[:, h * 128 : (h + 1) * 128]
+
+    for i, strips in enumerate((m_ref, o_ref)):
+        copies[i].wait()
+
+        def one(t, carry, i=i, strips=strips):
+            at = words[i, 0, t]
+            off = words[i, 1, t]
+            w = words[i, 2, t].astype(F32) * (1.0 / 256.0)
+            strip = strips[t].astype(F32) * w
+            for h in range(canvas.shape[1]):
+                canvas[at, h, pl.ds(off, th), :] += strip[:, h * 128 : (h + 1) * 128]
             return carry
 
-        lax.fori_loop(0, n, one, 0)
+        lax.fori_loop(0, n, one, 0, unroll=4)
     for h in range(canvas.shape[1]):
-        out_ref[:, :, h * 128 : (h + 1) * 128] = canvas[:, h].astype(BF16)
+        out_ref[:, :, h * 128 : (h + 1) * 128] = canvas[0:total, h].astype(BF16)
 
 
 def add_kernel(parts_ref, out_ref):
@@ -155,12 +171,12 @@
     column = as_column(jnp.maximum(summed[rows : rows + 1, 0:rows], 1.0))
     coadded = summed[0:rows] / column
     out_ref[...] = coadded
-    scaled_ref[...] = jnp.broadcast_to((gain_ref[0] * coadded)[None], scaled_ref.shape)
+    scaled_ref[...] = jnp.broadcast_to((gain_ref[0] * coadded).astype(BF16)[None], scaled_ref.shape)
     asked_ref[...] = summed[rows + 1 : rows + 2]
 
 
 def detect_kernel(bands_ref, asked_ref, det_ref, rows_ref):
-    detection = jnp.sum(bands_ref[...], axis=0)
+    detection = jnp.sum(bands_ref[...].astype(F32), axis=0)
     det_ref[...] = detection
     rows = det_ref.shape[0]
     ids = iota((rows, asked_ref.shape[1]), 0).astype(F32)
@@ -200,18 +216,21 @@
     rows = 2 * th
     high = rows + 8
     basis = coefs.shape[2]
-    depth = sky // 16
+    depth = sky // 8
     sky_of = lambda z, x, c: (z * 4 + x) * 2 + c
-    near = [[sky_of(2 * m + b, x, c) for b in range(2) for x in range(4)] for m in range(depth) for c in range(2)]
-    far = [[sky_of(2 * m + b, x, c) for m in range(depth)] for b in range(2) for x in range(4) for c in range(2)]
+    near = [[sky_of(z, x, c) for x in range(4)] for z in range(depth) for c in range(2)]
+    far = [[sky_of(z, x, c) for z in range(depth)] for x in range(4) for c in range(2)]
     partners = [(i, i ^ 1) for i in range(sky)]
-    me = lax.axis_index("sky").astype(I32)
-    here = jnp.stack([me & 1, 2 * (me & ~1)])
-
+    me = lax.axis_index("sky").astype(I32)[None]
+
+    inputs = (
+        tiles.reshape(n * th, cols), coefs[0].T, taps_rows[0], taps_cols[0],
+        tile_patch[:, :, 0], tile_offset, weight_index, weight_table, source_patch[:, :, 0], source_row,
+    )
     matched = pl.pallas_call(
         match_kernel,
         out_shape=SDS((n + 1, th, cols), BF16),
-        in_specs=[VM] * 10,
+        in_specs=[pl.BlockSpec(memory_space=pltpu.HBM)] * 10,
         out_specs=VM,
         scratch_shapes=[
             pltpu.VMEM((16, cols), F32),
@@ -219,13 +238,12 @@
             pltpu.VMEM((th, basis * th), BF16),
             pltpu.VMEM((n * th, 8), F32),
             pltpu.VMEM((256 // th, basis * th, cols), BF16),
-        ],
+        ]
+        + [pltpu.VMEM(v.shape, v.dtype) for v in inputs]
+        + [pltpu.SemaphoreType.DMA((len(inputs),))],
         name="match",
-        compiler_params=grant(10),
-    )(
-        tiles.reshape(n * th, cols), coefs[0].T, taps_rows[0], taps_cols[0],
-        tile_patch[:, :, 0], tile_offset, weight_index, weight_table, source_patch[:, :, 0], source_row,
-    )
+        compiler_params=grant(63),
+    )(*inputs)
     other = lax.ppermute(matched, "sky", partners)
 
     canvas = pl.pallas_call(
@@ -234,16 +252,16 @@
         in_specs=[SM, VM, VM],
         out_specs=VM,
         scratch_shapes=[
-            pltpu.VMEM((sky // 2, cols // 128, high, 128), F32),
+            pltpu.VMEM((sky // 2 + 1, cols // 128, high, 128), F32),
             pltpu.VMEM((2, 8, 128), I32),
             pltpu.SMEM((2, 8, 128), I32),
-            pltpu.SemaphoreType.DMA,
+            pltpu.SemaphoreType.DMA((2,)),
         ],
         name="place",
         compiler_params=grant(14),
-    )(here, matched, other)
-
-    along_x = exchange(canvas, near).reshape(8, depth, high, cols)
+    )(me, matched, other)
+
+    along_x = exchange(canvas, near).reshape(4, depth, high, cols)
     partial = pl.pallas_call(
         add_kernel, out_shape=SDS((depth, high, cols), BF16), in_specs=[VM], out_specs=VM, name="add",
         compiler_params=grant(8),
@@ -252,7 +270,7 @@
 
     coadded, scaled, asked = pl.pallas_call(
         coadd_kernel,
-        out_shape=(SDS((rows, cols), F32), SDS((band, rows, cols), F32), SDS((1, cols), F32)),
+        out_shape=(SDS((rows, cols), F32), SDS((band, rows, cols), BF16), SDS((1, cols), F32)),
         in_specs=[VM, SM],
         out_specs=(VM, VM, VM),
         name="coadd",

time: 132 us -> 135 us (1.023)
  blocking collectives: 67.5 us -> 74.2 us
  local copies, waits for them, and re-layouts: 7.31 us -> 1.35 us
  waiting for transfers between devices: 20.9 us -> 26.4 us
  Pallas kernels: 14.2 us -> 12.4 us
    all_to_all x3, blocking collectives: 67.5 us -> 74.2 us  [exchange(): lax.all_to_all(value, axis, split_axis=0, concat_axis=0, tiled=True, axis...]
    unnamed x24 -> x6, local copies, waits for them, and re-layouts: 7.2 us -> 1.24 us
    all_to_all x1, waiting for transfers between devices: 18.7 us -> 23.9 us  [exchange(): lax.all_to_all(value, axis, split_axis=0, concat_axis=0, tiled=True, axis...]
    pallas_call x1, Pallas kernels: 6.2 us -> 2.34 us  [per_device(): pl.pallas_call(place_kernel, out_shape=SDS((sky // 2, high, cols), BF16),...]
    pallas_call x1, Pallas kernels: 4.86 us -> 6.85 us  [per_device(): pl.pallas_call(match_kernel, out_shape=SDS((n + 1, th, cols), BF16), in_s...]
where the time goes in v3:
time: 135 us
  blocking collectives  74.2 us (55%)
  waiting for transfers between devices  26.4 us (20%)
  starting transfers between devices  19.1 us (14%)
  Pallas kernels  12.4 us (9%)
  local copies, waits for them, and re-layouts  1.35 us (1%)
  between operations  1.35 us (1%)
    all_to_all x3, blocking collectives, exchange(): lax.all_to_all(value, axis, split_axis=0, concat_axis=0, tiled=True, axis...  74.2 us
    all_to_all x1, waiting for transfers between devices, exchange(): lax.all_to_all(value, axis, split_axis=0, concat_axis=0, tiled=True, axis...  23.9 us
    all_to_all x1, starting transfers between devices, exchange(): lax.all_to_all(value, axis, split_axis=0, concat_axis=0, tiled=True, axis...  10.3 us
    ppermute x1, starting transfers between devices, per_device(): other = lax.ppermute(matched, 'sky', partners)  8.75 us
    pallas_call x1, Pallas kernels, per_device(): pl.pallas_call(match_kernel, out_shape=SDS((n + 1, th, cols), BF16), in_s...  6.85 us
  transfers between devices with their start and end apart: 2, of which 2 were waited for; matrix products, arithmetic and copies ran while one was open for 0% of the time, Pallas kernels for 0%

profile of v3, /device:TPU:1, one launch (start us, length us, event | category | flops | bytes accessed | tf_op | source)
XLA Modules:
  0.0 134.7 jit_solution(4949040361195833788)
XLA Ops:
  0.6 6.8 %match.1.m_ref = bf16[65,32,256]{2,1,0:T(8,128)(2,1)} custom-call(bf16[2048,256]{1,0:T(8,128)(2,1)} %bitcast.16, bf16[5,64]{1,0:T(8,128)(2,1)} %bitcast.17, bf16[5,41]{1,0:T(8,128)(2,1)} %bitcast.18, bf16[5,41]{1,0:T(8,128)(2,1)} %bitcast.19, s32[1,64]{1,0:T(1,128)} %bitcast.20, s32[1,64]{1,0:T(1,128)} %refs_5_.1, s32[1,64]{1,0:T(1,128)} %refs_6_.1, ...), custom_call_target="tpu_custom_call" | custom-call | tf_op jit(solution)/shard_map/match/pallas_call | solution.py:230
  7.5 8.7 %collective-permute-start = (bf16[65,32,256]{2,1,0:T(8,128)(2,1)}, bf16[65,32,256]{2,1,0:T(8,128)(2,1)S(1)}, u32[]{:S(2)}, u32[]{:S(2)}) collective-permute-start(bf16[65,32,256]{2,1,0:T(8,128)(2,1)} %match.1.m_ref), channel_id=1, source_target_pairs={{0,4},{4,0},{8,12},{12,8},{16,20},{20,16},{24,28},{28,24},{32,36},... | collective-permute-start | bytes 3194888 | tf_op jit(solution)/shard_map/ppermute | solution.py:247
  16.2 2.5 %collective-permute-done.o_ref = bf16[65,32,256]{2,1,0:T(8,128)(2,1)S(1)} collective-permute-done((bf16[65,32,256]{2,1,0:T(8,128)(2,1)}, bf16[65,32,256]{2,1,0:T(8,128)(2,1)S(1)}, u32[]{:S(2)}, u32[]{:S(2)}) %collective-permute-start) | collective-permute-done | bytes 1064992 | tf_op jit(solution)/shard_map/ppermute | solution.py:247
  18.7 0.0 copy-start
  18.7 1.2 copy-done
  20.0 2.3 %place.1 = bf16[64,72,256]{2,1,0:T(8,128)(2,1)S(1)} custom-call(s32[1]{0:T(128)} %bitcast.me_ref, bf16[65,32,256]{2,1,0:T(8,128)(2,1)S(1)} %copy-done, bf16[65,32,256]{2,1,0:T(8,128)(2,1)S(1)} %collective-permute-done.o_ref), custom_call_target="tpu_custom_call" | custom-call | tf_op jit(solution)/shard_map/place/pallas_call | solution.py:249
  22.3 31.3 %all_to_all.20 = bf16[64,72,256]{2,1,0:T(8,128)(2,1)S(1)} all-to-all(bf16[64,72,256]{2,1,0:T(8,128)(2,1)S(1)} %place.1), channel_id=1, replica_groups={{0,8,16,24},{4,12,20,28},{32,40,48,56},{36,44,52,60},{64,72,80,88},{68,..., dimensions={0} | all-to-all | bytes 4718592 | tf_op jit(solution)/shard_map/all_to_all | solution.py:206
  53.7 0.0 copy-start.1
  53.7 0.0 copy-start.2
  53.7 1.1 add.1
  54.8 10.3 %all-to-all-start.1 = ((bf16[16,72,256]{2,1,0:T(8,128)(2,1)}), bf16[16,72,256]{2,1,0:T(8,128)(2,1)S(1)}, u32[]{:S(2)}, u32[]{:S(2)}) async-start(bf16[16,72,256]{2,1,0:T(8,128)(2,1)} %add.1), calls=%async_computation.1 | async-start | bytes 1179648 | tf_op jit(solution)/shard_map/all_to_all | solution.py:206
  65.8 23.9 %all-to-all-done.1.parts_ref = bf16[16,72,256]{2,1,0:T(8,128)(2,1)S(1)} async-done(((bf16[16,72,256]{2,1,0:T(8,128)(2,1)}), bf16[16,72,256]{2,1,0:T(8,128)(2,1)S(1)}, u32[]{:S(2)}, u32[]{:S(2)}) %all-to-all-start.1) | async-done | bytes 589856 | tf_op jit(solution)/shard_map/all_to_all | solution.py:206
  89.6 0.7 coadd.1
  90.4 8.8 %all_to_all.21.bands_ref = bf16[4,64,256]{2,1,0:T(8,128)(2,1)S(1)} all-to-all(bf16[4,64,256]{2,1,0:T(8,128)(2,1)S(1)} %get-tuple-element.9), channel_id=1, replica_groups=mesh['sky'=128,'band'=4] {'band'}, dimensions={0} | all-to-all | bytes 262144 | tf_op jit(solution)/shard_map/all_to_all | solution.py:206
  99.2 0.7 detect.1
  99.8 0.1 reshape.20
  99.9 34.0 %all_to_all.22 = bf16[128,2,256]{2,1,0:T(2,128)(2,1)S(1)} all-to-all(bf16[128,2,256]{2,1,0:T(2,128)(2,1)S(1)} %reshape.20), channel_id=1, replica_groups=mesh['sky'=128,'band'=4] {'sky'}, dimensions={0} | all-to-all | bytes 262144 | tf_op jit(solution)/shard_map/all_to_all | solution.py:206
  133.9 0.1 reshape.21.rows_ref
  134.0 0.0 copy-done.1
  134.0 0.0 copy-done.2
  134.0 0.7 flux.1
Async XLA Ops:
  7.5 11.3 %collective-permute-start = (bf16[65,32,256]{2,1,0:T(8,128)(2,1)}, bf16[65,32,256]{2,1,0:T(8,128)(2,1)S(1)}, u32[]{:S(2)}, u32[]{:S(2)}) collective-permute-start(bf16[65,32,256]{2,1,0:T(8,128)(2,1)} %match.1.m_ref), channel_id=1, source_target_pairs={{0,4},{4,0},{8,12},{12,8},{16,20},{20,16},{24,28},{28,24},{32,36},... | collective-permute-start | bytes 3194888 | tf_op jit(solution)/shard_map/ppermute | solution.py:247
  18.7 1.2 copy-start
  53.7 80.3 %copy-start.1 = (bf16[1,64,256]{2,1,0:T(8,128)(2,1)S(1)}, bf16[1,64,256]{2,1,0:T(8,128)(2,1)}, u32[]{:S(2)}) copy-start(bf16[1,64,256]{2,1,0:T(8,128)(2,1)} %param.21) | copy-start | bytes 98308
  53.7 80.3 %copy-start.2 = (s32[1,64,1]{1,2,0:T(1,128)S(1)}, s32[1,64,1]{1,2,0:T(1,128)}, u32[]{:S(2)}) copy-start(s32[1,64,1]{1,2,0:T(1,128)} %param.22) | copy-start | bytes 772
  54.8 34.9 %all-to-all-start.1 = ((bf16[16,72,256]{2,1,0:T(8,128)(2,1)}), bf16[16,72,256]{2,1,0:T(8,128)(2,1)S(1)}, u32[]{:S(2)}, u32[]{:S(2)}) async-start(bf16[16,72,256]{2,1,0:T(8,128)(2,1)} %add.1), calls=%async_computation.1 | async-start | bytes 1179648 | tf_op jit(solution)/shard_map/all_to_all | solution.py:206

commit v4 on v3

--- a/solution.py
+++ b/solution.py
@@ -102,63 +102,75 @@
     lax.fori_loop(0, n // group, one_group, 0)
 
 
-def place_kernel(me_ref, m_ref, o_ref, out_ref, canvas, words_s, words, sem):
+def place_strips(me_ref, strips, sender, canvas, words_s, words, sem):
     core = me_ref[0] & 1
     first = 2 * (me_ref[0] - core)
-    n = m_ref.shape[0] - 1
-    th = m_ref.shape[1]
+    n = strips.shape[0] - 1
+    th = strips.shape[1]
     rows = 2 * th
-    total = out_ref.shape[0]
-    depth = total // 4
+    total = canvas.shape[0] - 1
+    depth = total // 8
 
     def place_of(patch):
         q = patch >> 1
         x, z = q & 3, q >> 2
-        return jnp.where((patch & 1) == core, x * depth + z, total)
-
-    coverage = jnp.zeros((total, 128), F32)
-    requests = jnp.zeros((total, 256), F32)
+        return jnp.where((patch & 1) == core, ((z & 1) * 4 + x) * depth + (z >> 1), total)
+
     lane = iota((n, 256), 1)
-    copies = []
-    for i, strips in enumerate((m_ref, o_ref)):
-        details = strips[n, 0:8, 0:128].astype(F32)[:, 0:n]
-        patch, offset, patch_s = (details[r : r + 1].astype(I32) for r in (0, 1, 3))
-        weight, row_s, rank_s = (details[r : r + 1] for r in (2, 4, 5))
-        at = place_of(patch)
-        words_s[i, 0:1, 0:n] = at
-        words_s[i, 1:2, 0:n] = offset
-        words_s[i, 2:3, 0:n] = (weight * 256.0).astype(I32)
-        copies.append(pltpu.make_async_copy(words_s.at[i], words.at[i], sem.at[i]))
-        copies[-1].start()
-        off_col = as_column(offset)
-        covered = (lane >= off_col) & (lane < off_col + th)
-        covers = jnp.where(covered, as_column(weight), 0.0)[:, 0:128].astype(BF16)
-        here = (iota((total, n), 0) == at).astype(F32).astype(BF16)
-        coverage += jnp.dot(here, covers, preferred_element_type=F32)
-        slot = rank_s.astype(I32) + (first + 2 * (core if i == 0 else 1 - core))
-        asks = jnp.where(lane == as_column(slot), as_column(row_s), 0.0).astype(BF16)
-        there = (iota((total, n), 0) == place_of(patch_s)).astype(F32).astype(BF16)
-        requests += jnp.dot(there, asks, preferred_element_type=F32)
+    details = strips[n, 0:8, 0:128].astype(F32)[:, 0:n]
+    patch, offset, patch_s = (details[r : r + 1].astype(I32) for r in (0, 1, 3))
+    weight, row_s, rank_s = (details[r : r + 1] for r in (2, 4, 5))
+    at = place_of(patch)
+    words_s[0:1, 0:n] = at
+    words_s[1:2, 0:n] = offset
+    words_s[2:3, 0:n] = (weight * 256.0).astype(I32)
+    copy = pltpu.make_async_copy(words_s, words, sem)
+    copy.start()
+    off_col = as_column(offset)
+    covered = (lane >= off_col) & (lane < off_col + th)
+    covers = jnp.where(covered, as_column(weight), 0.0)[:, 0:128].astype(BF16)
+    here = (iota((total, n), 0) == at).astype(F32).astype(BF16)
+    coverage = jnp.dot(here, covers, preferred_element_type=F32)
+    slot = rank_s.astype(I32) + (first + 2 * sender)
+    asks = jnp.where(lane == as_column(slot), as_column(row_s), 0.0).astype(BF16)
+    there = (iota((total, n), 0) == place_of(patch_s)).astype(F32).astype(BF16)
+    requests = jnp.dot(there, asks, preferred_element_type=F32)
+
+    def add_extras():
+        for r, value in ((0, coverage), (1, requests[:, 0:128]), (2, requests[:, 128:256])):
+            canvas[0:total, 2 * rows + r, :] = value
+
+    def add_strips():
+        copy.wait()
+
+        def one(t, carry):
+            at = words[0, t]
+            off = words[1, t]
+            w = words[2, t].astype(F32) * (1.0 / 256.0)
+            strip = strips[t].astype(F32) * w
+            for h in range(strip.shape[1] // 128):
+                canvas[at, pl.ds(h * rows + off, th), :] += strip[:, h * 128 : (h + 1) * 128]
+            return carry
+
+        lax.fori_loop(0, n, one, 0, unroll=4)
+
+    return add_extras, add_strips
+
+
+def place_own_kernel(me_ref, m_ref, canvas, words_s, words, sem):
+    add_extras, add_strips = place_strips(me_ref, m_ref, me_ref[0] & 1, canvas, words_s, words, sem)
     canvas[...] = jnp.zeros(canvas.shape, F32)
-    canvas[0:total, 0, rows, :] = coverage
-    for h in range(canvas.shape[1]):
-        canvas[0:total, h, rows + 1, :] = requests[:, h * 128 : (h + 1) * 128]
-
-    for i, strips in enumerate((m_ref, o_ref)):
-        copies[i].wait()
-
-        def one(t, carry, i=i, strips=strips):
-            at = words[i, 0, t]
-            off = words[i, 1, t]
-            w = words[i, 2, t].astype(F32) * (1.0 / 256.0)
-            strip = strips[t].astype(F32) * w
-            for h in range(canvas.shape[1]):
-                canvas[at, h, pl.ds(off, th), :] += strip[:, h * 128 : (h + 1) * 128]
-            return carry
-
-        lax.fori_loop(0, n, one, 0, unroll=4)
-    for h in range(canvas.shape[1]):
-        out_ref[:, :, h * 128 : (h + 1) * 128] = canvas[0:total, h].astype(BF16)
+    add_extras()
+    add_strips()
+
+
+def place_other_kernel(me_ref, o_ref, own_ref, out_ref, canvas, words_s, words, sem):
+    add_extras, add_strips = place_strips(me_ref, o_ref, 1 - (me_ref[0] & 1), canvas, words_s, words, sem)
+    canvas[...] = jnp.zeros(canvas.shape, F32)
+    add_extras()
+    add_strips()
+    total = out_ref.shape[0]
+    out_ref[...] = (own_ref[0:total] + canvas[0:total]).astype(BF16)
 
 
 def add_kernel(parts_ref, out_ref):
@@ -168,11 +180,14 @@
 def coadd_kernel(parts_ref, gain_ref, out_ref, scaled_ref, asked_ref):
     rows, cols = out_ref.shape
     summed = jnp.sum(parts_ref[...].astype(F32), axis=0)
-    column = as_column(jnp.maximum(summed[rows : rows + 1, 0:rows], 1.0))
-    coadded = summed[0:rows] / column
-    out_ref[...] = coadded
-    scaled_ref[...] = jnp.broadcast_to((gain_ref[0] * coadded).astype(BF16)[None], scaled_ref.shape)
-    asked_ref[...] = summed[rows + 1 : rows + 2]
+    column = as_column(jnp.maximum(summed[2 * rows : 2 * rows + 1, 0:rows], 1.0))
+    for h in range(cols // 128):
+        part = slice(h * 128, (h + 1) * 128)
+        coadded = summed[h * rows : (h + 1) * rows] / column
+        out_ref[:, part] = coadded
+        for b in range(scaled_ref.shape[0]):
+            scaled_ref[b, :, part] = (gain_ref[0] * coadded).astype(BF16)
+        asked_ref[:, part] = summed[2 * rows + 1 + h : 2 * rows + 2 + h]
 
 
 def detect_kernel(bands_ref, asked_ref, det_ref, rows_ref):
@@ -214,12 +229,12 @@
     band = lax.axis_size("band")
     _, n, th, cols = tiles.shape
     rows = 2 * th
-    high = rows + 8
+    high = rows * (cols // 128) + 8
     basis = coefs.shape[2]
-    depth = sky // 8
+    depth = sky // 16
     sky_of = lambda z, x, c: (z * 4 + x) * 2 + c
-    near = [[sky_of(z, x, c) for x in range(4)] for z in range(depth) for c in range(2)]
-    far = [[sky_of(z, x, c) for z in range(depth)] for x in range(4) for c in range(2)]
+    near = [[sky_of(2 * m + b, x, c) for b in range(2) for x in range(4)] for m in range(depth) for c in range(2)]
+    far = [[sky_of(2 * m + b, x, c) for m in range(depth)] for b in range(2) for x in range(4) for c in range(2)]
     partners = [(i, i ^ 1) for i in range(sky)]
     me = lax.axis_index("sky").astype(I32)[None]
 
@@ -246,24 +261,33 @@
     )(*inputs)
     other = lax.ppermute(matched, "sky", partners)
 
+    place_scratch = [pltpu.VMEM((8, 128), I32), pltpu.SMEM((8, 128), I32), pltpu.SemaphoreType.DMA]
+    own = pl.pallas_call(
+        place_own_kernel,
+        out_shape=SDS((sky // 2 + 1, high, 128), F32),
+        in_specs=[SM, VM],
+        out_specs=VM,
+        scratch_shapes=place_scratch,
+        name="place_own",
+        compiler_params=grant(4),
+    )(me, matched)
     canvas = pl.pallas_call(
-        place_kernel,
-        out_shape=SDS((sky // 2, high, cols), BF16),
+        place_other_kernel,
+        out_shape=SDS((sky // 2, high, 128), BF16),
         in_specs=[SM, VM, VM],
         out_specs=VM,
-        scratch_shapes=[
-            pltpu.VMEM((sky // 2 + 1, cols // 128, high, 128), F32),
-            pltpu.VMEM((2, 8, 128), I32),
-            pltpu.SMEM((2, 8, 128), I32),
-            pltpu.SemaphoreType.DMA((2,)),
-        ],
-        name="place",
-        compiler_params=grant(14),
-    )(me, matched, other)
-
-    along_x = exchange(canvas, near).reshape(4, depth, high, cols)
+        scratch_shapes=[pltpu.VMEM(own.shape, F32)] + place_scratch,
+        name="place_other",
+        compiler_params=grant(10),
+    )(me, other, own)
+
+    along_x = exchange(canvas, near).reshape(8, depth, high, 128)
     partial = pl.pallas_call(
-        add_kernel, out_shape=SDS((depth, high, cols), BF16), in_specs=[VM], out_specs=VM, name="add",
+        add_kernel,
+        out_shape=SDS((depth, high, 128), BF16),
+        in_specs=[VM],
+        out_specs=VM,
+        name="add",
         compiler_params=grant(8),
     )(along_x)
     along_z = exchange(partial, far)

time: 135 us -> 120 us (0.89)
  waiting for transfers between devices: 26.4 us -> 16.6 us
  blocking collectives: 74.2 us -> 66.9 us
    all_to_all x3, blocking collectives: 74.2 us -> 66.9 us  [exchange(): lax.all_to_all(value, axis, split_axis=0, concat_axis=0, tiled=True, axis...]
    all_to_all x1, waiting for transfers between devices: 23.9 us -> 16.6 us  [exchange(): lax.all_to_all(value, axis, split_axis=0, concat_axis=0, tiled=True, axis...]
    ppermute x1, waiting for transfers between devices: 2.49 us -> 0.01 us  [per_device(): other = lax.ppermute(matched, 'sky', partners)]
    pallas_call x2 -> x3, Pallas kernels: 3.44 us -> 4.23 us  [the longest x1 1.84 us: per_device(): pl.pallas_call(place_other_kernel, out_shape=SDS((sky // 2, high, 128), B...]
  transfers between devices with their start and end apart: 2 -> 2, of which waited for: 2 -> 1; matrix products, arithmetic and copies ran while one was open for 0% -> 0% of each run, Pallas kernels for 0% -> 1%
where the time goes in v4:
time: 120 us
  blocking collectives  66.9 us (56%)
  starting transfers between devices  20.1 us (17%)
  waiting for transfers between devices  16.6 us (14%)
  Pallas kernels  13.2 us (11%)
  between operations  1.36 us (1%)
  local copies, waits for them, and re-layouts  1.34 us (1%)
    all_to_all x3, blocking collectives, exchange(): lax.all_to_all(value, axis, split_axis=0, concat_axis=0, tiled=True, axis...  66.9 us
    all_to_all x1, waiting for transfers between devices, exchange(): lax.all_to_all(value, axis, split_axis=0, concat_axis=0, tiled=True, axis...  16.6 us
    all_to_all x1, starting transfers between devices, exchange(): lax.all_to_all(value, axis, split_axis=0, concat_axis=0, tiled=True, axis...  11.3 us
    ppermute x1, starting transfers between devices, per_device(): other = lax.ppermute(matched, 'sky', partners)  8.75 us
    pallas_call x1, Pallas kernels, per_device(): pl.pallas_call(match_kernel, out_shape=SDS((n + 1, th, cols), BF16), in_s...  6.85 us
  transfers between devices with their start and end apart: 2, of which 1 were waited for; matrix products, arithmetic and copies ran while one was open for 0% of the time, Pallas kernels for 1%

profile of v4, /device:TPU:1, one launch (start us, length us, event | category | flops | bytes accessed | tf_op | source)
XLA Modules:
  0.0 119.5 jit_solution(2367964239911253708)
XLA Ops:
  0.6 6.8 %match.1.m_ref = bf16[65,32,256]{2,1,0:T(8,128)(2,1)} custom-call(bf16[2048,256]{1,0:T(8,128)(2,1)} %bitcast.16, bf16[5,64]{1,0:T(8,128)(2,1)} %bitcast.17, bf16[5,41]{1,0:T(8,128)(2,1)} %bitcast.18, bf16[5,41]{1,0:T(8,128)(2,1)} %bitcast.19, s32[1,64]{1,0:T(1,128)} %bitcast.20, s32[1,64]{1,0:T(1,128)} %refs_5_.1, s32[1,64]{1,0:T(1,128)} %refs_6_.1, ...), custom_call_target="tpu_custom_call" | custom-call | tf_op jit(solution)/shard_map/match/pallas_call | solution.py:245
  7.5 8.7 %collective-permute-start = (bf16[65,32,256]{2,1,0:T(8,128)(2,1)}, bf16[65,32,256]{2,1,0:T(8,128)(2,1)S(1)}, u32[]{:S(2)}, u32[]{:S(2)}) collective-permute-start(bf16[65,32,256]{2,1,0:T(8,128)(2,1)} %match.1.m_ref), channel_id=1, source_target_pairs={{0,4},{4,0},{8,12},{12,8},{16,20},{20,16},{24,28},{28,24},{32,36},... | collective-permute-start | bytes 3194888 | tf_op jit(solution)/shard_map/ppermute | solution.py:262
  16.2 0.0 copy-start
  16.3 1.2 %copy-done = bf16[65,32,256]{2,1,0:T(8,128)(2,1)S(1)} copy-done((bf16[65,32,256]{2,1,0:T(8,128)(2,1)S(1)}, bf16[65,32,256]{2,1,0:T(8,128)(2,1)}, u32[]{:S(2)}) %copy-start) | copy-done | bytes 1064984
  17.5 1.4 %place_own.1.own_ref = f32[65,136,128]{2,1,0:T(8,128)S(1)} custom-call(s32[1]{0:T(128)} %bitcast.me_ref, bf16[65,32,256]{2,1,0:T(8,128)(2,1)S(1)} %copy-done), custom_call_target="tpu_custom_call" | custom-call | tf_op jit(solution)/shard_map/place_own/pallas_call | solution.py:265
  18.9 0.0 collective-permute-done.o_ref
  18.9 1.8 %place_other.1 = bf16[64,136,128]{2,1,0:T(8,128)(2,1)S(1)} custom-call(s32[1]{0:T(128)} %bitcast.me_ref, bf16[65,32,256]{2,1,0:T(8,128)(2,1)S(1)} %collective-permute-done.o_ref, f32[65,136,128]{2,1,0:T(8,128)S(1)} %place_own.1.own_ref), custom_call_target="tpu_custom_call" | custom-call | tf_op jit(solution)/shard_map/place_other/pallas_call | solution.py:274
  20.8 30.0 %all_to_all.20 = bf16[64,136,128]{2,1,0:T(8,128)(2,1)S(1)} all-to-all(bf16[64,136,128]{2,1,0:T(8,128)(2,1)S(1)} %place_other.1), channel_id=1, replica_groups={{0,8,16,24,32,40,48,56},{4,12,20,28,36,44,52,60},{64,72,80,88,96,104,11..., dimensions={0} | all-to-all | bytes 4456448 | tf_op jit(solution)/shard_map/all_to_all | solution.py:221
  50.8 0.0 copy-start.1
  50.8 0.0 copy-start.2
  50.8 1.0 add.1
  51.7 11.3 %all-to-all-start.1 = ((bf16[8,136,128]{2,1,0:T(8,128)(2,1)}), bf16[8,136,128]{2,1,0:T(8,128)(2,1)S(1)}, u32[]{:S(2)}, u32[]{:S(2)}) async-start(bf16[8,136,128]{2,1,0:T(8,128)(2,1)} %add.1), calls=%async_computation.1 | async-start | bytes 557056 | tf_op jit(solution)/shard_map/all_to_all | solution.py:221
  63.7 16.6 %all-to-all-done.1.parts_ref = bf16[8,136,128]{2,1,0:T(8,128)(2,1)S(1)} async-done(((bf16[8,136,128]{2,1,0:T(8,128)(2,1)}), bf16[8,136,128]{2,1,0:T(8,128)(2,1)S(1)}, u32[]{:S(2)}, u32[]{:S(2)}) %all-to-all-start.1) | async-done | bytes 278560 | tf_op jit(solution)/shard_map/all_to_all | solution.py:221
  80.3 0.7 coadd.1
  81.1 8.8 %all_to_all.21.bands_ref = bf16[4,64,256]{2,1,0:T(8,128)(2,1)S(1)} all-to-all(bf16[4,64,256]{2,1,0:T(8,128)(2,1)S(1)} %get-tuple-element.9), channel_id=1, replica_groups=mesh['sky'=128,'band'=4] {'band'}, dimensions={0} | all-to-all | bytes 262144 | tf_op jit(solution)/shard_map/all_to_all | solution.py:221
  89.9 0.7 detect.1
  90.5 0.1 reshape.20
  90.6 28.1 %all_to_all.22 = bf16[128,2,256]{2,1,0:T(2,128)(2,1)S(1)} all-to-all(bf16[128,2,256]{2,1,0:T(2,128)(2,1)S(1)} %reshape.20), channel_id=1, replica_groups=mesh['sky'=128,'band'=4] {'sky'}, dimensions={0} | all-to-all | bytes 262144 | tf_op jit(solution)/shard_map/all_to_all | solution.py:221
  118.7 0.1 reshape.21.rows_ref
  118.8 0.0 copy-done.1
  118.8 0.0 copy-done.2
  118.8 0.7 flux.1
Async XLA Ops:
  7.5 11.4 %collective-permute-start = (bf16[65,32,256]{2,1,0:T(8,128)(2,1)}, bf16[65,32,256]{2,1,0:T(8,128)(2,1)S(1)}, u32[]{:S(2)}, u32[]{:S(2)}) collective-permute-start(bf16[65,32,256]{2,1,0:T(8,128)(2,1)} %match.1.m_ref), channel_id=1, source_target_pairs={{0,4},{4,0},{8,12},{12,8},{16,20},{20,16},{24,28},{28,24},{32,36},... | collective-permute-start | bytes 3194888 | tf_op jit(solution)/shard_map/ppermute | solution.py:262
  16.2 1.2 %copy-start = (bf16[65,32,256]{2,1,0:T(8,128)(2,1)S(1)}, bf16[65,32,256]{2,1,0:T(8,128)(2,1)}, u32[]{:S(2)}) copy-start(bf16[65,32,256]{2,1,0:T(8,128)(2,1)} %match.1.m_ref) | copy-start | bytes 3194884
  50.8 68.0 %copy-start.1 = (bf16[1,64,256]{2,1,0:T(8,128)(2,1)S(1)}, bf16[1,64,256]{2,1,0:T(8,128)(2,1)}, u32[]{:S(2)}) copy-start(bf16[1,64,256]{2,1,0:T(8,128)(2,1)} %param.21) | copy-start | bytes 98308
  50.8 68.0 %copy-start.2 = (s32[1,64,1]{1,2,0:T(1,128)S(1)}, s32[1,64,1]{1,2,0:T(1,128)}, u32[]{:S(2)}) copy-start(s32[1,64,1]{1,2,0:T(1,128)} %param.22) | copy-start | bytes 772
  51.7 28.6 %all-to-all-start.1 = ((bf16[8,136,128]{2,1,0:T(8,128)(2,1)}), bf16[8,136,128]{2,1,0:T(8,128)(2,1)S(1)}, u32[]{:S(2)}, u32[]{:S(2)}) async-start(bf16[8,136,128]{2,1,0:T(8,128)(2,1)} %add.1), calls=%async_computation.1 | async-start | bytes 557056 | tf_op jit(solution)/shard_map/all_to_all | solution.py:221

commit v5 on v4

--- a/solution.py
+++ b/solution.py
@@ -42,36 +42,28 @@
 
 
 def match_kernel(*refs):
-    sources, out_ref, scratch = refs[:10], refs[10], refs[11:]
-    inner, held, sems = scratch[:5], scratch[5:15], scratch[15]
+    sources, sent_ref, scratch = refs[:10], refs[10], refs[11:]
+    taps_s, v_s, u_s, c_s, a_s, out_s = scratch[:6]
+    held, sems, out_sems = scratch[6:16], scratch[16], scratch[17]
+    tiles_ref, coef_ref, tr_ref, tc_ref = held[:4]
     copies = [pltpu.make_async_copy(src, dst, sems.at[i]) for i, (src, dst) in enumerate(zip(sources, held))]
-    for copy in copies[::-1]:
-        copy.start()
-    for copy in copies[1:]:
-        copy.wait()
-    match_body(copies[0], *held, out_ref, *inner)
-
-
-def match_body(
-    tiles_copy, tiles_ref, coef_ref, tr_ref, tc_ref, tp_ref, to_ref, wi_ref, wt_ref, sp_ref, sr_ref,
-    out_ref, taps_s, v_s, u_s, ce_s, a_s,
-):
-    write_details(out_ref, tp_ref, to_ref, wi_ref, wt_ref, sp_ref, sr_ref)
+    for i in (3, 2, 1, 0, 4, 5, 6, 7, 8, 9):
+        copies[i].start()
+
     basis, tap_total = tc_ref.shape
     half = (tap_total - 1) // 2
     cols = tiles_ref.shape[1]
-    th = out_ref.shape[1]
+    th = out_s.shape[1]
+    n = coef_ref.shape[1]
     group = 256 // th
     taps_s[...] = jnp.zeros(taps_s.shape, F32)
+    lag = iota((cols, cols), 1) - iota((cols, cols), 0)
+    inside = (lag >= -half) & (lag <= half)
+    copies[3].wait()
+    copies[2].wait()
     taps_s[0:basis, 0:tap_total] = tc_ref[...].astype(F32)
     taps_s[8 : 8 + basis, 0:tap_total] = tr_ref[...].astype(F32)
     taps_s[...] = pltpu.roll(taps_s[...], cols - half, 1)
-    lag = iota((cols, cols), 1) - iota((cols, cols), 0)
-    inside = (lag >= -half) & (lag <= half)
-    for k in range(basis):
-        rows = jnp.broadcast_to(taps_s[k : k + 1, :], (cols, cols))
-        rolled = pltpu.roll(rows, 0, 1, stride=1, stride_axis=0)
-        v_s[k] = jnp.where(inside, rolled, 0.0).astype(BF16)
     parts = []
     for k in range(basis):
         rows = jnp.broadcast_to(taps_s[8 + k : 9 + k, :], (th, cols))
@@ -80,26 +72,45 @@
     parts.append(jnp.zeros((256 - basis * th, 128), F32))
     vertical = jnp.concatenate(parts, axis=0).T
     u_s[...] = vertical[0:th, 0 : basis * th].astype(BF16)
-    n = coef_ref.shape[1]
-    spread = (iota((n * th, n), 0) // th == iota((n * th, n), 1)).astype(F32).astype(BF16)
-    ce_s[:, 0:basis] = lax.dot_general(spread, coef_ref[...], NT, preferred_element_type=F32)
-
-    tiles_copy.wait()
+    for k in range(basis):
+        rows = jnp.broadcast_to(taps_s[k : k + 1, :], (cols, cols))
+        rolled = pltpu.roll(rows, 0, 1, stride=1, stride_axis=0)
+        v_s[k] = jnp.where(inside, rolled, 0.0).astype(BF16)
+    copies[1].wait()
+    for k in range(basis):
+        choose = (iota((basis, cols), 0) == k).astype(F32).astype(BF16)
+        c_s[k] = lax.dot_general(coef_ref[...], choose, TN, preferred_element_type=F32)
+    for i in range(4, 10):
+        copies[i].wait()
+    write_details(out_s, *held[4:])
+    last = pltpu.make_async_copy(out_s.at[n], sent_ref.at[n], out_sems.at[n // group])
+    last.start()
+    copies[0].wait()
+
+    def block(g):
+        return pltpu.make_async_copy(
+            out_s.at[pl.ds(g * group, group)], sent_ref.at[pl.ds(g * group, group)], out_sems.at[g]
+        )
 
     def one_group(g, carry):
         start = pl.multiple_of(g * 256, 256)
         pixels = tiles_ref[pl.ds(start, 256), :]
-        coef = ce_s[pl.ds(start, 256), :]
         for k in range(basis):
             across = jnp.dot(pixels, v_s[k], preferred_element_type=F32)
-            across = (across * coef[:, k : k + 1]).astype(BF16)
-            a_s[:, k * th : (k + 1) * th, :] = across.reshape(group, th, cols)
+            for t in range(group):
+                coef = c_s[k, pl.ds(g * group + t, 1), :]
+                part = across[t * th : (t + 1) * th] * coef
+                a_s[g % 2, t, k * th : (k + 1) * th, :] = part.astype(BF16)
         for t in range(group):
-            done = jnp.dot(u_s[...], a_s[t], preferred_element_type=F32)
-            out_ref[g * group + t] = done.astype(BF16)
+            done = jnp.dot(u_s[...], a_s[g % 2, t], preferred_element_type=F32)
+            out_s[g * group + t] = done.astype(BF16)
+        block(g).start()
         return carry
 
-    lax.fori_loop(0, n // group, one_group, 0)
+    lax.fori_loop(0, n // group, one_group, 0, unroll=UNROLL)
+    for g in range(n // group):
+        block(g).wait()
+    last.wait()
 
 
 def place_strips(me_ref, strips, sender, canvas, words_s, words, sem):
@@ -208,6 +219,7 @@
     out_ref[...] = jnp.sum(jnp.where(wanted, each, 0.0), axis=0, keepdims=True)
 
 
+UNROLL = 2
 VM = pl.BlockSpec(memory_space=pltpu.VMEM)
 SM = pl.BlockSpec(memory_space=pltpu.SMEM)
 SDS = jax.ShapeDtypeStruct
@@ -246,16 +258,17 @@
         match_kernel,
         out_shape=SDS((n + 1, th, cols), BF16),
         in_specs=[pl.BlockSpec(memory_space=pltpu.HBM)] * 10,
-        out_specs=VM,
+        out_specs=pl.BlockSpec(memory_space=pltpu.HBM),
         scratch_shapes=[
             pltpu.VMEM((16, cols), F32),
             pltpu.VMEM((basis, cols, cols), BF16),
             pltpu.VMEM((th, basis * th), BF16),
-            pltpu.VMEM((n * th, 8), F32),
-            pltpu.VMEM((256 // th, basis * th, cols), BF16),
+            pltpu.VMEM((basis, n, cols), F32),
+            pltpu.VMEM((2, 256 // th, basis * th, cols), BF16),
+            pltpu.VMEM((n + 1, th, cols), BF16),
         ]
         + [pltpu.VMEM(v.shape, v.dtype) for v in inputs]
-        + [pltpu.SemaphoreType.DMA((len(inputs),))],
+        + [pltpu.SemaphoreType.DMA((len(inputs),)), pltpu.SemaphoreType.DMA((n * th // 256 + 1,))],
         name="match",
         compiler_params=grant(63),
     )(*inputs)

time: 120 us -> 119 us (level)
  no operation moved by 1% of the time
where the time goes in v5:
time: 119 us; the launch traced here: 118 us
  blocking collectives  66.9 us (56%)
  starting transfers between devices  20.1 us (17%)
  waiting for transfers between devices  16.6 us (14%)
  Pallas kernels  12.1 us (10%)
  between operations  1.36 us (1%)
  local copies, waits for them, and re-layouts  1.34 us (1%)
    all_to_all x3, blocking collectives, exchange(): lax.all_to_all(value, axis, split_axis=0, concat_axis=0, tiled=True, axis...  66.9 us
    all_to_all x1, waiting for transfers between devices, exchange(): lax.all_to_all(value, axis, split_axis=0, concat_axis=0, tiled=True, axis...  16.6 us
    all_to_all x1, starting transfers between devices, exchange(): lax.all_to_all(value, axis, split_axis=0, concat_axis=0, tiled=True, axis...  11.3 us
    ppermute x1, starting transfers between devices, per_device(): other = lax.ppermute(matched, 'sky', partners)  8.75 us
    pallas_call x1, Pallas kernels, per_device(): pl.pallas_call(match_kernel, out_shape=SDS((n + 1, th, cols), BF16), in_s...  5.79 us
  transfers between devices with their start and end apart: 2, of which 1 were waited for; matrix products, arithmetic and copies ran while one was open for 0% of the time, Pallas kernels for 1%

profile of v5, /device:TPU:1, one launch (start us, length us, event | category | flops | bytes accessed | tf_op | source)
XLA Modules:
  0.0 118.5 jit_solution(17897086818260233341)
XLA Ops:
  0.6 5.8 %match.1.m_ref = bf16[65,32,256]{2,1,0:T(8,128)(2,1)} custom-call(bf16[2048,256]{1,0:T(8,128)(2,1)} %bitcast.16, bf16[5,64]{1,0:T(8,128)(2,1)} %bitcast.17, bf16[5,41]{1,0:T(8,128)(2,1)} %bitcast.18, bf16[5,41]{1,0:T(8,128)(2,1)} %bitcast.19, s32[1,64]{1,0:T(1,128)} %bitcast.20, s32[1,64]{1,0:T(1,128)} %refs_5_.1, s32[1,64]{1,0:T(1,128)} %refs_6_.1, ...), custom_call_target="tpu_custom_call" | custom-call | tf_op jit(solution)/shard_map/match/pallas_call | solution.py:257
  6.4 8.7 %collective-permute-start = (bf16[65,32,256]{2,1,0:T(8,128)(2,1)}, bf16[65,32,256]{2,1,0:T(8,128)(2,1)S(1)}, u32[]{:S(2)}, u32[]{:S(2)}) collective-permute-start(bf16[65,32,256]{2,1,0:T(8,128)(2,1)} %match.1.m_ref), channel_id=1, source_target_pairs={{0,4},{4,0},{8,12},{12,8},{16,20},{20,16},{24,28},{28,24},{32,36},... | collective-permute-start | bytes 3194888 | tf_op jit(solution)/shard_map/ppermute | solution.py:275
  15.2 0.0 copy-start
  15.2 1.2 %copy-done = bf16[65,32,256]{2,1,0:T(8,128)(2,1)S(1)} copy-done((bf16[65,32,256]{2,1,0:T(8,128)(2,1)S(1)}, bf16[65,32,256]{2,1,0:T(8,128)(2,1)}, u32[]{:S(2)}) %copy-start) | copy-done | bytes 1064984
  16.4 1.4 %place_own.1.own_ref = f32[65,136,128]{2,1,0:T(8,128)S(1)} custom-call(s32[1]{0:T(128)} %bitcast.me_ref, bf16[65,32,256]{2,1,0:T(8,128)(2,1)S(1)} %copy-done), custom_call_target="tpu_custom_call" | custom-call | tf_op jit(solution)/shard_map/place_own/pallas_call | solution.py:278
  17.8 0.0 collective-permute-done.o_ref
  17.8 1.8 %place_other.1 = bf16[64,136,128]{2,1,0:T(8,128)(2,1)S(1)} custom-call(s32[1]{0:T(128)} %bitcast.me_ref, bf16[65,32,256]{2,1,0:T(8,128)(2,1)S(1)} %collective-permute-done.o_ref, f32[65,136,128]{2,1,0:T(8,128)S(1)} %place_own.1.own_ref), custom_call_target="tpu_custom_call" | custom-call | tf_op jit(solution)/shard_map/place_other/pallas_call | solution.py:287
  19.7 30.0 %all_to_all.20 = bf16[64,136,128]{2,1,0:T(8,128)(2,1)S(1)} all-to-all(bf16[64,136,128]{2,1,0:T(8,128)(2,1)S(1)} %place_other.1), channel_id=1, replica_groups={{0,8,16,24,32,40,48,56},{4,12,20,28,36,44,52,60},{64,72,80,88,96,104,11..., dimensions={0} | all-to-all | bytes 4456448 | tf_op jit(solution)/shard_map/all_to_all | solution.py:233
  49.7 0.0 copy-start.1
  49.7 0.0 copy-start.2
  49.7 1.0 add.1
  50.7 11.3 %all-to-all-start.1 = ((bf16[8,136,128]{2,1,0:T(8,128)(2,1)}), bf16[8,136,128]{2,1,0:T(8,128)(2,1)S(1)}, u32[]{:S(2)}, u32[]{:S(2)}) async-start(bf16[8,136,128]{2,1,0:T(8,128)(2,1)} %add.1), calls=%async_computation.1 | async-start | bytes 557056 | tf_op jit(solution)/shard_map/all_to_all | solution.py:233
  62.7 16.6 %all-to-all-done.1.parts_ref = bf16[8,136,128]{2,1,0:T(8,128)(2,1)S(1)} async-done(((bf16[8,136,128]{2,1,0:T(8,128)(2,1)}), bf16[8,136,128]{2,1,0:T(8,128)(2,1)S(1)}, u32[]{:S(2)}, u32[]{:S(2)}) %all-to-all-start.1) | async-done | bytes 278560 | tf_op jit(solution)/shard_map/all_to_all | solution.py:233
  79.3 0.7 coadd.1
  80.0 8.8 %all_to_all.21.bands_ref = bf16[4,64,256]{2,1,0:T(8,128)(2,1)S(1)} all-to-all(bf16[4,64,256]{2,1,0:T(8,128)(2,1)S(1)} %get-tuple-element.9), channel_id=1, replica_groups=mesh['sky'=128,'band'=4] {'band'}, dimensions={0} | all-to-all | bytes 262144 | tf_op jit(solution)/shard_map/all_to_all | solution.py:233
  88.8 0.7 detect.1
  89.5 0.1 reshape.20
  89.5 28.1 %all_to_all.22 = bf16[128,2,256]{2,1,0:T(2,128)(2,1)S(1)} all-to-all(bf16[128,2,256]{2,1,0:T(2,128)(2,1)S(1)} %reshape.20), channel_id=1, replica_groups=mesh['sky'=128,'band'=4] {'sky'}, dimensions={0} | all-to-all | bytes 262144 | tf_op jit(solution)/shard_map/all_to_all | solution.py:233
  117.7 0.1 reshape.21.rows_ref
  117.7 0.0 copy-done.1
  117.7 0.0 copy-done.2
  117.8 0.7 flux.1
Async XLA Ops:
  6.4 11.4 %collective-permute-start = (bf16[65,32,256]{2,1,0:T(8,128)(2,1)}, bf16[65,32,256]{2,1,0:T(8,128)(2,1)S(1)}, u32[]{:S(2)}, u32[]{:S(2)}) collective-permute-start(bf16[65,32,256]{2,1,0:T(8,128)(2,1)} %match.1.m_ref), channel_id=1, source_target_pairs={{0,4},{4,0},{8,12},{12,8},{16,20},{20,16},{24,28},{28,24},{32,36},... | collective-permute-start | bytes 3194888 | tf_op jit(solution)/shard_map/ppermute | solution.py:275
  15.2 1.2 %copy-start = (bf16[65,32,256]{2,1,0:T(8,128)(2,1)S(1)}, bf16[65,32,256]{2,1,0:T(8,128)(2,1)}, u32[]{:S(2)}) copy-start(bf16[65,32,256]{2,1,0:T(8,128)(2,1)} %match.1.m_ref) | copy-start | bytes 3194884
  49.7 68.0 %copy-start.1 = (bf16[1,64,256]{2,1,0:T(8,128)(2,1)S(1)}, bf16[1,64,256]{2,1,0:T(8,128)(2,1)}, u32[]{:S(2)}) copy-start(bf16[1,64,256]{2,1,0:T(8,128)(2,1)} %param.21) | copy-start | bytes 98308
  49.7 68.1 %copy-start.2 = (s32[1,64,1]{1,2,0:T(1,128)S(1)}, s32[1,64,1]{1,2,0:T(1,128)}, u32[]{:S(2)}) copy-start(s32[1,64,1]{1,2,0:T(1,128)} %param.22) | copy-start | bytes 772
  50.7 28.6 %all-to-all-start.1 = ((bf16[8,136,128]{2,1,0:T(8,128)(2,1)}), bf16[8,136,128]{2,1,0:T(8,128)(2,1)S(1)}, u32[]{:S(2)}, u32[]{:S(2)}) async-start(bf16[8,136,128]{2,1,0:T(8,128)(2,1)} %add.1), calls=%async_computation.1 | async-start | bytes 557056 | tf_op jit(solution)/shard_map/all_to_all | solution.py:233

commit v6 on v5

--- a/solution.py
+++ b/solution.py
@@ -124,8 +124,10 @@
 
     def place_of(patch):
         q = patch >> 1
-        x, z = q & 3, q >> 2
-        return jnp.where((patch & 1) == core, ((z & 1) * 4 + x) * depth + (z >> 1), total)
+        x, z = (q + core) & 3, ((q >> 2) + core) & (2 * depth - 1)
+        pair = x >> 1
+        member = (z & 1) * 2 + ((x ^ pair) & 1)
+        return jnp.where((patch & 1) == core, (member * 2 + pair) * depth + (z >> 1), total)
 
     lane = iota((n, 256), 1)
     details = strips[n, 0:8, 0:128].astype(F32)[:, 0:n]
@@ -184,8 +186,15 @@
     out_ref[...] = (own_ref[0:total] + canvas[0:total]).astype(BF16)
 
 
-def add_kernel(parts_ref, out_ref):
-    out_ref[...] = jnp.sum(parts_ref[...].astype(F32), axis=0).astype(BF16)
+def split_kernel(me_ref, parts_ref, keep_ref, send_ref):
+    pair = (((me_ref[0] >> 1) + (me_ref[0] & 1)) & 3) >> 1
+    members = range(parts_ref.shape[0])
+    send_ref[...] = sum(parts_ref[s, 1 - pair].astype(F32) for s in members).astype(BF16)
+    keep_ref[...] = sum(parts_ref[s, pair].astype(F32) for s in members)
+
+
+def add_kernel(keep_ref, got_ref, out_ref):
+    out_ref[...] = (keep_ref[...] + got_ref[...].astype(F32)).astype(BF16)
 
 
 def coadd_kernel(parts_ref, gain_ref, out_ref, scaled_ref, asked_ref):
@@ -245,8 +254,15 @@
     basis = coefs.shape[2]
     depth = sky // 16
     sky_of = lambda z, x, c: (z * 4 + x) * 2 + c
-    near = [[sky_of(2 * m + b, x, c) for b in range(2) for x in range(4)] for m in range(depth) for c in range(2)]
-    far = [[sky_of(2 * m + b, x, c) for m in range(depth)] for b in range(2) for x in range(4) for c in range(2)]
+    device = lambda c, x, z: sky_of((z - c) % (2 * depth), (x - c) % 4, c)
+    spots = [(c, m) for c in range(2) for m in range(depth)]
+    near = [
+        [device(c, (3 * g) ^ e, 2 * m + b) for b in range(2) for e in range(2)] for c, m in spots for g in range(2)
+    ]
+    cross = [(device(c, x, z), device(c, 3 - x, z)) for c in range(2) for x in range(4) for z in range(2 * depth)]
+    far = [
+        [device(c, x, 2 * m + b) for m in range(depth)] for c in range(2) for b in range(2) for x in range(4)
+    ]
     partners = [(i, i ^ 1) for i in range(sky)]
     me = lax.axis_index("sky").astype(I32)[None]
 
@@ -294,15 +310,23 @@
         compiler_params=grant(10),
     )(me, other, own)
 
-    along_x = exchange(canvas, near).reshape(8, depth, high, 128)
+    along_x = exchange(canvas, near).reshape(4, 2, depth, high, 128)
+    keep, send = pl.pallas_call(
+        split_kernel,
+        out_shape=(SDS((depth, high, 128), F32), SDS((depth, high, 128), BF16)),
+        in_specs=[SM, VM],
+        out_specs=(VM, VM),
+        name="split",
+        compiler_params=grant(8),
+    )(me, along_x)
     partial = pl.pallas_call(
         add_kernel,
         out_shape=SDS((depth, high, 128), BF16),
-        in_specs=[VM],
+        in_specs=[VM, VM],
         out_specs=VM,
         name="add",
         compiler_params=grant(8),
-    )(along_x)
+    )(keep, lax.ppermute(send, "sky", cross))
     along_z = exchange(partial, far)
 
     coadded, scaled, asked = pl.pallas_call(

time: 119 us -> 116 us (0.975)
  blocking collectives: 66.9 us -> 61.3 us
  waiting for transfers between devices: 16.6 us -> 21.4 us
  starting transfers between devices: 20.1 us -> 17.8 us
    all_to_all x3, blocking collectives: 66.9 us -> 61.3 us  [exchange(): lax.all_to_all(value, axis, split_axis=0, concat_axis=0, tiled=True, axis...]
    ppermute x0 -> x1, waiting for transfers between devices: none -> 5.36 us  [per_device(): lax.ppermute(send, 'sky', cross)]
    all_to_all x1, starting transfers between devices: 11.3 us -> 7.16 us  [exchange(): lax.all_to_all(value, axis, split_axis=0, concat_axis=0, tiled=True, axis...]
    ppermute x0 -> x1, starting transfers between devices: none -> 1.92 us  [per_device(): lax.ppermute(send, 'sky', cross)]
  transfers between devices with their start and end apart: 2 -> 3, of which waited for: 1 -> 2; matrix products, arithmetic and copies ran while one was open for 0% -> 0% of each run, Pallas kernels for 1% -> 1%
where the time goes in v6:
time: 116 us
  blocking collectives  61.3 us (53%)
  waiting for transfers between devices  21.4 us (18%)
  starting transfers between devices  17.8 us (15%)
  Pallas kernels  12.2 us (11%)
  between operations  1.38 us (1%)
  local copies, waits for them, and re-layouts  1.34 us (1%)
    all_to_all x3, blocking collectives, exchange(): lax.all_to_all(value, axis, split_axis=0, concat_axis=0, tiled=True, axis...  61.3 us
    all_to_all x1, waiting for transfers between devices, exchange(): lax.all_to_all(value, axis, split_axis=0, concat_axis=0, tiled=True, axis...  16.1 us
    ppermute x1, starting transfers between devices, per_device(): other = lax.ppermute(matched, 'sky', partners)  8.75 us
    all_to_all x1, starting transfers between devices, exchange(): lax.all_to_all(value, axis, split_axis=0, concat_axis=0, tiled=True, axis...  7.16 us
    pallas_call x1, Pallas kernels, per_device(): pl.pallas_call(match_kernel, out_shape=SDS((n + 1, th, cols), BF16), in_s...  5.79 us
    ppermute x1, waiting for transfers between devices, per_device(): lax.ppermute(send, 'sky', cross)  5.36 us
  transfers between devices with their start and end apart: 3, of which 2 were waited for; matrix products, arithmetic and copies ran while one was open for 0% of the time, Pallas kernels for 1%

profile of v6, /device:TPU:1, one launch (start us, length us, event | category | flops | bytes accessed | tf_op | source)
XLA Modules:
  0.0 115.5 jit_solution(9576766501427365229)
XLA Ops:
  0.6 5.8 %match.1.m_ref = bf16[65,32,256]{2,1,0:T(8,128)(2,1)} custom-call(bf16[2048,256]{1,0:T(8,128)(2,1)} %bitcast.16, bf16[5,64]{1,0:T(8,128)(2,1)} %bitcast.17, bf16[5,41]{1,0:T(8,128)(2,1)} %bitcast.18, bf16[5,41]{1,0:T(8,128)(2,1)} %bitcast.19, s32[1,64]{1,0:T(1,128)} %bitcast.20, s32[1,64]{1,0:T(1,128)} %refs_5_.1, s32[1,64]{1,0:T(1,128)} %refs_6_.1, ...), custom_call_target="tpu_custom_call" | custom-call | tf_op jit(solution)/shard_map/match/pallas_call | solution.py:273
  6.4 8.7 %collective-permute-start = (bf16[65,32,256]{2,1,0:T(8,128)(2,1)}, bf16[65,32,256]{2,1,0:T(8,128)(2,1)S(1)}, u32[]{:S(2)}, u32[]{:S(2)}) collective-permute-start(bf16[65,32,256]{2,1,0:T(8,128)(2,1)} %match.1.m_ref), channel_id=1, source_target_pairs={{0,4},{4,0},{8,12},{12,8},{16,20},{20,16},{24,28},{28,24},{32,36},... | collective-permute-start | bytes 3194888 | tf_op jit(solution)/shard_map/ppermute | solution.py:291
  15.2 0.0 copy-start
  15.2 1.2 %copy-done = bf16[65,32,256]{2,1,0:T(8,128)(2,1)S(1)} copy-done((bf16[65,32,256]{2,1,0:T(8,128)(2,1)S(1)}, bf16[65,32,256]{2,1,0:T(8,128)(2,1)}, u32[]{:S(2)}) %copy-start) | copy-done | bytes 1064984
  16.4 1.4 %place_own.1.own_ref = f32[65,136,128]{2,1,0:T(8,128)S(1)} custom-call(s32[1]{0:T(128)} %bitcast.me_ref, bf16[65,32,256]{2,1,0:T(8,128)(2,1)S(1)} %copy-done), custom_call_target="tpu_custom_call" | custom-call | tf_op jit(solution)/shard_map/place_own/pallas_call | solution.py:294
  17.8 0.0 collective-permute-done.o_ref
  17.9 1.8 %place_other.1 = bf16[64,136,128]{2,1,0:T(8,128)(2,1)S(1)} custom-call(s32[1]{0:T(128)} %bitcast.me_ref, bf16[65,32,256]{2,1,0:T(8,128)(2,1)S(1)} %collective-permute-done.o_ref, f32[65,136,128]{2,1,0:T(8,128)S(1)} %place_own.1.own_ref), custom_call_target="tpu_custom_call" | custom-call | tf_op jit(solution)/shard_map/place_other/pallas_call | solution.py:303
  19.7 21.9 %all_to_all.20 = bf16[64,136,128]{2,1,0:T(8,128)(2,1)S(1)} all-to-all(bf16[64,136,128]{2,1,0:T(8,128)(2,1)S(1)} %place_other.1), channel_id=1, replica_groups={{0,8,32,40},{24,16,56,48},{64,72,96,104},{88,80,120,112},{128,136,160,1..., dimensions={0} | all-to-all | bytes 4456448 | tf_op jit(solution)/shard_map/all_to_all | solution.py:242
  41.6 0.0 copy-start.1
  41.6 0.3 split.1
  41.9 1.9 %collective-permute-start.1 = (bf16[8,136,128]{2,1,0:T(8,128)(2,1)S(1)}, bf16[8,136,128]{2,1,0:T(8,128)(2,1)S(1)}, u32[]{:S(2)}, u32[]{:S(2)}) collective-permute-start(bf16[8,136,128]{2,1,0:T(8,128)(2,1)S(1)} %get-tuple-element.11), channel_id=1, source_target_pairs={{0,24},{32,56},{64,88},{96,120},{128,152},{160,184},{192,216},{224... | collective-permute-start | bytes 835592 | tf_op jit(solution)/shard_map/ppermute | solution.py:329
  43.8 5.4 %collective-permute-done.1.got_ref = bf16[8,136,128]{2,1,0:T(8,128)(2,1)S(1)} collective-permute-done((bf16[8,136,128]{2,1,0:T(8,128)(2,1)S(1)}, bf16[8,136,128]{2,1,0:T(8,128)(2,1)S(1)}, u32[]{:S(2)}, u32[]{:S(2)}) %collective-permute-start.1) | collective-permute-done | bytes 278560 | tf_op jit(solution)/shard_map/ppermute | solution.py:329
  49.2 0.8 add.1
  50.0 7.2 %all-to-all-start.1 = ((bf16[8,136,128]{2,1,0:T(8,128)(2,1)}), bf16[8,136,128]{2,1,0:T(8,128)(2,1)S(1)}, u32[]{:S(2)}, u32[]{:S(2)}) async-start(bf16[8,136,128]{2,1,0:T(8,128)(2,1)} %add.1), calls=%async_computation.1 | async-start | bytes 557056 | tf_op jit(solution)/shard_map/all_to_all | solution.py:242
  57.8 16.1 %all-to-all-done.1.parts_ref = bf16[8,136,128]{2,1,0:T(8,128)(2,1)S(1)} async-done(((bf16[8,136,128]{2,1,0:T(8,128)(2,1)}), bf16[8,136,128]{2,1,0:T(8,128)(2,1)S(1)}, u32[]{:S(2)}, u32[]{:S(2)}) %all-to-all-start.1) | async-done | bytes 278560 | tf_op jit(solution)/shard_map/all_to_all | solution.py:242
  73.8 0.7 coadd.1
  74.6 8.8 %all_to_all.21.bands_ref = bf16[4,64,256]{2,1,0:T(8,128)(2,1)S(1)} all-to-all(bf16[4,64,256]{2,1,0:T(8,128)(2,1)S(1)} %get-tuple-element.13), channel_id=1, replica_groups=mesh['sky'=128,'band'=4] {'band'}, dimensions={0} | all-to-all | bytes 262144 | tf_op jit(solution)/shard_map/all_to_all | solution.py:242
  83.4 0.7 detect.1
  84.0 0.1 reshape.20
  84.1 30.6 %all_to_all.22 = bf16[128,2,256]{2,1,0:T(2,128)(2,1)S(1)} all-to-all(bf16[128,2,256]{2,1,0:T(2,128)(2,1)S(1)} %reshape.20), channel_id=1, replica_groups=mesh['sky'=128,'band'=4] {'sky'}, dimensions={0} | all-to-all | bytes 262144 | tf_op jit(solution)/shard_map/all_to_all | solution.py:242
  114.7 0.1 reshape.21.rows_ref
  114.8 0.0 copy-done.1
  114.8 0.0 copy-done.2
  114.8 0.7 flux.1
  (1 shorter events, 0.0 us)
Async XLA Ops:
  6.4 11.4 %collective-permute-start = (bf16[65,32,256]{2,1,0:T(8,128)(2,1)}, bf16[65,32,256]{2,1,0:T(8,128)(2,1)S(1)}, u32[]{:S(2)}, u32[]{:S(2)}) collective-permute-start(bf16[65,32,256]{2,1,0:T(8,128)(2,1)} %match.1.m_ref), channel_id=1, source_target_pairs={{0,4},{4,0},{8,12},{12,8},{16,20},{20,16},{24,28},{28,24},{32,36},... | collective-permute-start | bytes 3194888 | tf_op jit(solution)/shard_map/ppermute | solution.py:291
  15.2 1.2 %copy-start = (bf16[65,32,256]{2,1,0:T(8,128)(2,1)S(1)}, bf16[65,32,256]{2,1,0:T(8,128)(2,1)}, u32[]{:S(2)}) copy-start(bf16[65,32,256]{2,1,0:T(8,128)(2,1)} %match.1.m_ref) | copy-start | bytes 3194884
  41.6 73.2 %copy-start.1 = (bf16[1,64,256]{2,1,0:T(8,128)(2,1)S(1)}, bf16[1,64,256]{2,1,0:T(8,128)(2,1)}, u32[]{:S(2)}) copy-start(bf16[1,64,256]{2,1,0:T(8,128)(2,1)} %param.21) | copy-start | bytes 98308
  41.6 73.2 %copy-start.2 = (s32[1,64,1]{1,2,0:T(1,128)S(1)}, s32[1,64,1]{1,2,0:T(1,128)}, u32[]{:S(2)}) copy-start(s32[1,64,1]{1,2,0:T(1,128)} %param.22) | copy-start | bytes 772
  41.9 7.3 %collective-permute-start.1 = (bf16[8,136,128]{2,1,0:T(8,128)(2,1)S(1)}, bf16[8,136,128]{2,1,0:T(8,128)(2,1)S(1)}, u32[]{:S(2)}, u32[]{:S(2)}) collective-permute-start(bf16[8,136,128]{2,1,0:T(8,128)(2,1)S(1)} %get-tuple-element.11), channel_id=1, source_target_pairs={{0,24},{32,56},{64,88},{96,120},{128,152},{160,184},{192,216},{224... | collective-permute-start | bytes 835592 | tf_op jit(solution)/shard_map/ppermute | solution.py:329
  50.0 23.9 %all-to-all-start.1 = ((bf16[8,136,128]{2,1,0:T(8,128)(2,1)}), bf16[8,136,128]{2,1,0:T(8,128)(2,1)S(1)}, u32[]{:S(2)}, u32[]{:S(2)}) async-start(bf16[8,136,128]{2,1,0:T(8,128)(2,1)} %add.1), calls=%async_computation.1 | async-start | bytes 557056 | tf_op jit(solution)/shard_map/all_to_all | solution.py:242

commit v7 on v6

--- a/solution.py
+++ b/solution.py
@@ -92,22 +92,26 @@
             out_s.at[pl.ds(g * group, group)], sent_ref.at[pl.ds(g * group, group)], out_sems.at[g]
         )
 
-    def one_group(g, carry):
-        start = pl.multiple_of(g * 256, 256)
-        pixels = tiles_ref[pl.ds(start, 256), :]
-        for k in range(basis):
-            across = jnp.dot(pixels, v_s[k], preferred_element_type=F32)
+    def two_groups(i, carry):
+        for u in range(2):
+            g = 2 * i + u
+            start = pl.multiple_of(g * 256, 256)
+            pixels = tiles_ref[pl.ds(start, 256), :]
+            for k in range(basis):
+                across = jnp.dot(pixels, v_s[k], preferred_element_type=F32)
+                for t in range(group):
+                    coef = c_s[k, pl.ds(g * group + t, 1), :]
+                    part = across[t * th : (t + 1) * th] * coef
+                    a_s[u, t, k * th : (k + 1) * th, :] = part.astype(BF16)
+        for u in range(2):
+            g = 2 * i + u
             for t in range(group):
-                coef = c_s[k, pl.ds(g * group + t, 1), :]
-                part = across[t * th : (t + 1) * th] * coef
-                a_s[g % 2, t, k * th : (k + 1) * th, :] = part.astype(BF16)
-        for t in range(group):
-            done = jnp.dot(u_s[...], a_s[g % 2, t], preferred_element_type=F32)
-            out_s[g * group + t] = done.astype(BF16)
-        block(g).start()
+                done = jnp.dot(u_s[...], a_s[u, t], preferred_element_type=F32)
+                out_s[g * group + t] = done.astype(BF16)
+            block(g).start()
         return carry
 
-    lax.fori_loop(0, n // group, one_group, 0, unroll=UNROLL)
+    lax.fori_loop(0, n // group // 2, two_groups, 0)
     for g in range(n // group):
         block(g).wait()
     last.wait()
@@ -228,7 +232,6 @@
     out_ref[...] = jnp.sum(jnp.where(wanted, each, 0.0), axis=0, keepdims=True)
 
 
-UNROLL = 2
 VM = pl.BlockSpec(memory_space=pltpu.VMEM)
 SM = pl.BlockSpec(memory_space=pltpu.SMEM)
 SDS = jax.ShapeDtypeStruct

time: 116 us -> 115 us (level)
  no operation moved by 1% of the time
where the time goes in v7:
time: 115 us
  blocking collectives  61.4 us (53%)
  waiting for transfers between devices  21.4 us (19%)
  starting transfers between devices  17.8 us (15%)
  Pallas kernels  11.4 us (10%)
  between operations  1.38 us (1%)
  local copies, waits for them, and re-layouts  1.34 us (1%)
    all_to_all x3, blocking collectives, exchange(): lax.all_to_all(value, axis, split_axis=0, concat_axis=0, tiled=True, axis...  61.4 us
    all_to_all x1, waiting for transfers between devices, exchange(): lax.all_to_all(value, axis, split_axis=0, concat_axis=0, tiled=True, axis...  16.1 us
    ppermute x1, starting transfers between devices, per_device(): other = lax.ppermute(matched, 'sky', partners)  8.75 us
    all_to_all x1, starting transfers between devices, exchange(): lax.all_to_all(value, axis, split_axis=0, concat_axis=0, tiled=True, axis...  7.17 us
    ppermute x1, waiting for transfers between devices, per_device(): lax.ppermute(send, 'sky', cross)  5.36 us
    pallas_call x1, Pallas kernels, per_device(): pl.pallas_call(match_kernel, out_shape=SDS((n + 1, th, cols), BF16), in_s...  5.01 us
  transfers between devices with their start and end apart: 3, of which 2 were waited for; matrix products, arithmetic and copies ran while one was open for 0% of the time, Pallas kernels for 1%

profile of v7, /device:TPU:1, one launch (start us, length us, event | category | flops | bytes accessed | tf_op | source)
XLA Modules:
  0.0 114.7 jit_solution(8452863905391642532)
XLA Ops:
  0.6 5.0 %match.1.m_ref = bf16[65,32,256]{2,1,0:T(8,128)(2,1)} custom-call(bf16[2048,256]{1,0:T(8,128)(2,1)} %bitcast.16, bf16[5,64]{1,0:T(8,128)(2,1)} %bitcast.17, bf16[5,41]{1,0:T(8,128)(2,1)} %bitcast.18, bf16[5,41]{1,0:T(8,128)(2,1)} %bitcast.19, s32[1,64]{1,0:T(1,128)} %bitcast.20, s32[1,64]{1,0:T(1,128)} %refs_5_.1, s32[1,64]{1,0:T(1,128)} %refs_6_.1, ...), custom_call_target="tpu_custom_call" | custom-call | tf_op jit(solution)/shard_map/match/pallas_call | solution.py:276
  5.6 8.7 %collective-permute-start = (bf16[65,32,256]{2,1,0:T(8,128)(2,1)}, bf16[65,32,256]{2,1,0:T(8,128)(2,1)S(1)}, u32[]{:S(2)}, u32[]{:S(2)}) collective-permute-start(bf16[65,32,256]{2,1,0:T(8,128)(2,1)} %match.1.m_ref), channel_id=1, source_target_pairs={{0,4},{4,0},{8,12},{12,8},{16,20},{20,16},{24,28},{28,24},{32,36},... | collective-permute-start | bytes 3194888 | tf_op jit(solution)/shard_map/ppermute | solution.py:294
  14.4 0.0 copy-start
  14.4 1.2 %copy-done = bf16[65,32,256]{2,1,0:T(8,128)(2,1)S(1)} copy-done((bf16[65,32,256]{2,1,0:T(8,128)(2,1)S(1)}, bf16[65,32,256]{2,1,0:T(8,128)(2,1)}, u32[]{:S(2)}) %copy-start) | copy-done | bytes 1064984
  15.6 1.4 %place_own.1.own_ref = f32[65,136,128]{2,1,0:T(8,128)S(1)} custom-call(s32[1]{0:T(128)} %bitcast.me_ref, bf16[65,32,256]{2,1,0:T(8,128)(2,1)S(1)} %copy-done), custom_call_target="tpu_custom_call" | custom-call | tf_op jit(solution)/shard_map/place_own/pallas_call | solution.py:297
  17.1 0.0 collective-permute-done.o_ref
  17.1 1.8 %place_other.1 = bf16[64,136,128]{2,1,0:T(8,128)(2,1)S(1)} custom-call(s32[1]{0:T(128)} %bitcast.me_ref, bf16[65,32,256]{2,1,0:T(8,128)(2,1)S(1)} %collective-permute-done.o_ref, f32[65,136,128]{2,1,0:T(8,128)S(1)} %place_own.1.own_ref), custom_call_target="tpu_custom_call" | custom-call | tf_op jit(solution)/shard_map/place_other/pallas_call | solution.py:306
  18.9 21.9 %all_to_all.20 = bf16[64,136,128]{2,1,0:T(8,128)(2,1)S(1)} all-to-all(bf16[64,136,128]{2,1,0:T(8,128)(2,1)S(1)} %place_other.1), channel_id=1, replica_groups={{0,8,32,40},{24,16,56,48},{64,72,96,104},{88,80,120,112},{128,136,160,1..., dimensions={0} | all-to-all | bytes 4456448 | tf_op jit(solution)/shard_map/all_to_all | solution.py:245
  40.8 0.0 copy-start.1
  40.8 0.3 split.1
  41.1 1.9 %collective-permute-start.1 = (bf16[8,136,128]{2,1,0:T(8,128)(2,1)S(1)}, bf16[8,136,128]{2,1,0:T(8,128)(2,1)S(1)}, u32[]{:S(2)}, u32[]{:S(2)}) collective-permute-start(bf16[8,136,128]{2,1,0:T(8,128)(2,1)S(1)} %get-tuple-element.11), channel_id=1, source_target_pairs={{0,24},{32,56},{64,88},{96,120},{128,152},{160,184},{192,216},{224... | collective-permute-start | bytes 835592 | tf_op jit(solution)/shard_map/ppermute | solution.py:332
  43.0 5.4 %collective-permute-done.1.got_ref = bf16[8,136,128]{2,1,0:T(8,128)(2,1)S(1)} collective-permute-done((bf16[8,136,128]{2,1,0:T(8,128)(2,1)S(1)}, bf16[8,136,128]{2,1,0:T(8,128)(2,1)S(1)}, u32[]{:S(2)}, u32[]{:S(2)}) %collective-permute-start.1) | collective-permute-done | bytes 278560 | tf_op jit(solution)/shard_map/ppermute | solution.py:332
  48.4 0.8 add.1
  49.1 7.2 %all-to-all-start.1 = ((bf16[8,136,128]{2,1,0:T(8,128)(2,1)}), bf16[8,136,128]{2,1,0:T(8,128)(2,1)S(1)}, u32[]{:S(2)}, u32[]{:S(2)}) async-start(bf16[8,136,128]{2,1,0:T(8,128)(2,1)} %add.1), calls=%async_computation.1 | async-start | bytes 557056 | tf_op jit(solution)/shard_map/all_to_all | solution.py:245
  57.0 16.1 %all-to-all-done.1.parts_ref = bf16[8,136,128]{2,1,0:T(8,128)(2,1)S(1)} async-done(((bf16[8,136,128]{2,1,0:T(8,128)(2,1)}), bf16[8,136,128]{2,1,0:T(8,128)(2,1)S(1)}, u32[]{:S(2)}, u32[]{:S(2)}) %all-to-all-start.1) | async-done | bytes 278560 | tf_op jit(solution)/shard_map/all_to_all | solution.py:245
  73.0 0.7 coadd.1
  73.8 8.8 %all_to_all.21.bands_ref = bf16[4,64,256]{2,1,0:T(8,128)(2,1)S(1)} all-to-all(bf16[4,64,256]{2,1,0:T(8,128)(2,1)S(1)} %get-tuple-element.13), channel_id=1, replica_groups=mesh['sky'=128,'band'=4] {'band'}, dimensions={0} | all-to-all | bytes 262144 | tf_op jit(solution)/shard_map/all_to_all | solution.py:245
  82.6 0.7 detect.1
  83.2 0.1 reshape.20
  83.3 30.6 %all_to_all.22 = bf16[128,2,256]{2,1,0:T(2,128)(2,1)S(1)} all-to-all(bf16[128,2,256]{2,1,0:T(2,128)(2,1)S(1)} %reshape.20), channel_id=1, replica_groups=mesh['sky'=128,'band'=4] {'sky'}, dimensions={0} | all-to-all | bytes 262144 | tf_op jit(solution)/shard_map/all_to_all | solution.py:245
  113.9 0.1 reshape.21.rows_ref
  114.0 0.0 copy-done.1
  114.0 0.0 copy-done.2
  114.0 0.7 flux.1
  (1 shorter events, 0.0 us)
Async XLA Ops:
  5.6 11.4 %collective-permute-start = (bf16[65,32,256]{2,1,0:T(8,128)(2,1)}, bf16[65,32,256]{2,1,0:T(8,128)(2,1)S(1)}, u32[]{:S(2)}, u32[]{:S(2)}) collective-permute-start(bf16[65,32,256]{2,1,0:T(8,128)(2,1)} %match.1.m_ref), channel_id=1, source_target_pairs={{0,4},{4,0},{8,12},{12,8},{16,20},{20,16},{24,28},{28,24},{32,36},... | collective-permute-start | bytes 3194888 | tf_op jit(solution)/shard_map/ppermute | solution.py:294
  14.4 1.2 %copy-start = (bf16[65,32,256]{2,1,0:T(8,128)(2,1)S(1)}, bf16[65,32,256]{2,1,0:T(8,128)(2,1)}, u32[]{:S(2)}) copy-start(bf16[65,32,256]{2,1,0:T(8,128)(2,1)} %match.1.m_ref) | copy-start | bytes 3194884
  40.8 73.2 %copy-start.1 = (bf16[1,64,256]{2,1,0:T(8,128)(2,1)S(1)}, bf16[1,64,256]{2,1,0:T(8,128)(2,1)}, u32[]{:S(2)}) copy-start(bf16[1,64,256]{2,1,0:T(8,128)(2,1)} %param.21) | copy-start | bytes 98308
  40.8 73.2 %copy-start.2 = (s32[1,64,1]{1,2,0:T(1,128)S(1)}, s32[1,64,1]{1,2,0:T(1,128)}, u32[]{:S(2)}) copy-start(s32[1,64,1]{1,2,0:T(1,128)} %param.22) | copy-start | bytes 772
  41.1 7.3 %collective-permute-start.1 = (bf16[8,136,128]{2,1,0:T(8,128)(2,1)S(1)}, bf16[8,136,128]{2,1,0:T(8,128)(2,1)S(1)}, u32[]{:S(2)}, u32[]{:S(2)}) collective-permute-start(bf16[8,136,128]{2,1,0:T(8,128)(2,1)S(1)} %get-tuple-element.11), channel_id=1, source_target_pairs={{0,24},{32,56},{64,88},{96,120},{128,152},{160,184},{192,216},{224... | collective-permute-start | bytes 835592 | tf_op jit(solution)/shard_map/ppermute | solution.py:332
  49.1 23.9 %all-to-all-start.1 = ((bf16[8,136,128]{2,1,0:T(8,128)(2,1)}), bf16[8,136,128]{2,1,0:T(8,128)(2,1)S(1)}, u32[]{:S(2)}, u32[]{:S(2)}) async-start(bf16[8,136,128]{2,1,0:T(8,128)(2,1)} %add.1), calls=%async_computation.1 | async-start | bytes 557056 | tf_op jit(solution)/shard_map/all_to_all | solution.py:245

commit v8 on v7

--- a/solution.py
+++ b/solution.py
@@ -128,9 +128,9 @@
 
     def place_of(patch):
         q = patch >> 1
-        x, z = (q + core) & 3, ((q >> 2) + core) & (2 * depth - 1)
+        x, z = (q + core) & 3, q >> 2
         pair = x >> 1
-        member = (z & 1) * 2 + ((x ^ pair) & 1)
+        member = ((z + core) & 1) * 2 + ((x ^ pair) & 1)
         return jnp.where((patch & 1) == core, (member * 2 + pair) * depth + (z >> 1), total)
 
     lane = iota((n, 256), 1)
@@ -263,9 +263,7 @@
         [device(c, (3 * g) ^ e, 2 * m + b) for b in range(2) for e in range(2)] for c, m in spots for g in range(2)
     ]
     cross = [(device(c, x, z), device(c, 3 - x, z)) for c in range(2) for x in range(4) for z in range(2 * depth)]
-    far = [
-        [device(c, x, 2 * m + b) for m in range(depth)] for c in range(2) for b in range(2) for x in range(4)
-    ]
+    far = [[sky_of(2 * m + b, x, c) for m in range(depth)] for b in range(2) for x in range(4) for c in range(2)]
     partners = [(i, i ^ 1) for i in range(sky)]
     me = lax.axis_index("sky").astype(I32)[None]
 

time: 115 us -> 115 us (level)
  blocking collectives: 61.4 us -> 59.8 us
    all_to_all x3, blocking collectives: 61.4 us -> 59.8 us  [exchange(): lax.all_to_all(value, axis, split_axis=0, concat_axis=0, tiled=True, axis...]
where the time goes in v8:
time: 115 us; the launch traced here: 114 us
  blocking collectives  59.8 us (52%)
  waiting for transfers between devices  22.5 us (20%)
  starting transfers between devices  17.8 us (15%)
  Pallas kernels  11.4 us (10%)
  between operations  1.38 us (1%)
  local copies, waits for them, and re-layouts  1.34 us (1%)
    all_to_all x3, blocking collectives, exchange(): lax.all_to_all(value, axis, split_axis=0, concat_axis=0, tiled=True, axis...  59.8 us
    all_to_all x1, waiting for transfers between devices, exchange(): lax.all_to_all(value, axis, split_axis=0, concat_axis=0, tiled=True, axis...  17.1 us
    ppermute x1, starting transfers between devices, per_device(): other = lax.ppermute(matched, 'sky', partners)  8.75 us
    all_to_all x1, starting transfers between devices, exchange(): lax.all_to_all(value, axis, split_axis=0, concat_axis=0, tiled=True, axis...  7.17 us
    ppermute x1, waiting for transfers between devices, per_device(): lax.ppermute(send, 'sky', cross)  5.36 us
    pallas_call x1, Pallas kernels, per_device(): pl.pallas_call(match_kernel, out_shape=SDS((n + 1, th, cols), BF16), in_s...  5.01 us
  transfers between devices with their start and end apart: 3, of which 2 were waited for; matrix products, arithmetic and copies ran while one was open for 0% of the time, Pallas kernels for 1%

profile of v8, /device:TPU:1, one launch (start us, length us, event | category | flops | bytes accessed | tf_op | source)
XLA Modules:
  0.0 114.2 jit_solution(4820516286035393963)
XLA Ops:
  0.6 5.0 %match.1.m_ref = bf16[65,32,256]{2,1,0:T(8,128)(2,1)} custom-call(bf16[2048,256]{1,0:T(8,128)(2,1)} %bitcast.16, bf16[5,64]{1,0:T(8,128)(2,1)} %bitcast.17, bf16[5,41]{1,0:T(8,128)(2,1)} %bitcast.18, bf16[5,41]{1,0:T(8,128)(2,1)} %bitcast.19, s32[1,64]{1,0:T(1,128)} %bitcast.20, s32[1,64]{1,0:T(1,128)} %refs_5_.1, s32[1,64]{1,0:T(1,128)} %refs_6_.1, ...), custom_call_target="tpu_custom_call" | custom-call | tf_op jit(solution)/shard_map/match/pallas_call | solution.py:274
  5.6 8.7 %collective-permute-start = (bf16[65,32,256]{2,1,0:T(8,128)(2,1)}, bf16[65,32,256]{2,1,0:T(8,128)(2,1)S(1)}, u32[]{:S(2)}, u32[]{:S(2)}) collective-permute-start(bf16[65,32,256]{2,1,0:T(8,128)(2,1)} %match.1.m_ref), channel_id=1, source_target_pairs={{0,4},{4,0},{8,12},{12,8},{16,20},{20,16},{24,28},{28,24},{32,36},... | collective-permute-start | bytes 3194888 | tf_op jit(solution)/shard_map/ppermute | solution.py:292
  14.4 0.0 copy-start
  14.4 1.2 %copy-done = bf16[65,32,256]{2,1,0:T(8,128)(2,1)S(1)} copy-done((bf16[65,32,256]{2,1,0:T(8,128)(2,1)S(1)}, bf16[65,32,256]{2,1,0:T(8,128)(2,1)}, u32[]{:S(2)}) %copy-start) | copy-done | bytes 1064984
  15.6 1.4 %place_own.1.own_ref = f32[65,136,128]{2,1,0:T(8,128)S(1)} custom-call(s32[1]{0:T(128)} %bitcast.me_ref, bf16[65,32,256]{2,1,0:T(8,128)(2,1)S(1)} %copy-done), custom_call_target="tpu_custom_call" | custom-call | tf_op jit(solution)/shard_map/place_own/pallas_call | solution.py:295
  17.1 0.0 collective-permute-done.o_ref
  17.1 1.8 %place_other.1 = bf16[64,136,128]{2,1,0:T(8,128)(2,1)S(1)} custom-call(s32[1]{0:T(128)} %bitcast.me_ref, bf16[65,32,256]{2,1,0:T(8,128)(2,1)S(1)} %collective-permute-done.o_ref, f32[65,136,128]{2,1,0:T(8,128)S(1)} %place_own.1.own_ref), custom_call_target="tpu_custom_call" | custom-call | tf_op jit(solution)/shard_map/place_other/pallas_call | solution.py:304
  18.9 21.9 %all_to_all.20 = bf16[64,136,128]{2,1,0:T(8,128)(2,1)S(1)} all-to-all(bf16[64,136,128]{2,1,0:T(8,128)(2,1)S(1)} %place_other.1), channel_id=1, replica_groups={{0,8,32,40},{24,16,56,48},{64,72,96,104},{88,80,120,112},{128,136,160,1..., dimensions={0} | all-to-all | bytes 4456448 | tf_op jit(solution)/shard_map/all_to_all | solution.py:245
  40.8 0.0 copy-start.1
  40.8 0.3 split.1
  41.1 1.9 %collective-permute-start.1 = (bf16[8,136,128]{2,1,0:T(8,128)(2,1)S(1)}, bf16[8,136,128]{2,1,0:T(8,128)(2,1)S(1)}, u32[]{:S(2)}, u32[]{:S(2)}) collective-permute-start(bf16[8,136,128]{2,1,0:T(8,128)(2,1)S(1)} %get-tuple-element.11), channel_id=1, source_target_pairs={{0,24},{32,56},{64,88},{96,120},{128,152},{160,184},{192,216},{224... | collective-permute-start | bytes 835592 | tf_op jit(solution)/shard_map/ppermute | solution.py:330
  43.0 5.4 %collective-permute-done.1.got_ref = bf16[8,136,128]{2,1,0:T(8,128)(2,1)S(1)} collective-permute-done((bf16[8,136,128]{2,1,0:T(8,128)(2,1)S(1)}, bf16[8,136,128]{2,1,0:T(8,128)(2,1)S(1)}, u32[]{:S(2)}, u32[]{:S(2)}) %collective-permute-start.1) | collective-permute-done | bytes 278560 | tf_op jit(solution)/shard_map/ppermute | solution.py:330
  48.4 0.8 add.1
  49.2 7.2 %all-to-all-start.1 = ((bf16[8,136,128]{2,1,0:T(8,128)(2,1)}), bf16[8,136,128]{2,1,0:T(8,128)(2,1)S(1)}, u32[]{:S(2)}, u32[]{:S(2)}) async-start(bf16[8,136,128]{2,1,0:T(8,128)(2,1)} %add.1), calls=%async_computation.1 | async-start | bytes 557056 | tf_op jit(solution)/shard_map/all_to_all | solution.py:245
  57.0 17.1 %all-to-all-done.1.parts_ref = bf16[8,136,128]{2,1,0:T(8,128)(2,1)S(1)} async-done(((bf16[8,136,128]{2,1,0:T(8,128)(2,1)}), bf16[8,136,128]{2,1,0:T(8,128)(2,1)S(1)}, u32[]{:S(2)}, u32[]{:S(2)}) %all-to-all-start.1) | async-done | bytes 278560 | tf_op jit(solution)/shard_map/all_to_all | solution.py:245
  74.1 0.7 coadd.1
  74.9 8.8 %all_to_all.21.bands_ref = bf16[4,64,256]{2,1,0:T(8,128)(2,1)S(1)} all-to-all(bf16[4,64,256]{2,1,0:T(8,128)(2,1)S(1)} %get-tuple-element.13), channel_id=1, replica_groups=mesh['sky'=128,'band'=4] {'band'}, dimensions={0} | all-to-all | bytes 262144 | tf_op jit(solution)/shard_map/all_to_all | solution.py:245
  83.7 0.7 detect.1
  84.3 0.1 reshape.20
  84.4 29.1 %all_to_all.22 = bf16[128,2,256]{2,1,0:T(2,128)(2,1)S(1)} all-to-all(bf16[128,2,256]{2,1,0:T(2,128)(2,1)S(1)} %reshape.20), channel_id=1, replica_groups=mesh['sky'=128,'band'=4] {'sky'}, dimensions={0} | all-to-all | bytes 262144 | tf_op jit(solution)/shard_map/all_to_all | solution.py:245
  113.5 0.1 reshape.21.rows_ref
  113.5 0.0 copy-done.1
  113.5 0.0 copy-done.2
  113.5 0.7 flux.1
  (1 shorter events, 0.0 us)
Async XLA Ops:
  5.6 11.4 %collective-permute-start = (bf16[65,32,256]{2,1,0:T(8,128)(2,1)}, bf16[65,32,256]{2,1,0:T(8,128)(2,1)S(1)}, u32[]{:S(2)}, u32[]{:S(2)}) collective-permute-start(bf16[65,32,256]{2,1,0:T(8,128)(2,1)} %match.1.m_ref), channel_id=1, source_target_pairs={{0,4},{4,0},{8,12},{12,8},{16,20},{20,16},{24,28},{28,24},{32,36},... | collective-permute-start | bytes 3194888 | tf_op jit(solution)/shard_map/ppermute | solution.py:292
  14.4 1.2 %copy-start = (bf16[65,32,256]{2,1,0:T(8,128)(2,1)S(1)}, bf16[65,32,256]{2,1,0:T(8,128)(2,1)}, u32[]{:S(2)}) copy-start(bf16[65,32,256]{2,1,0:T(8,128)(2,1)} %match.1.m_ref) | copy-start | bytes 3194884
  40.8 72.7 %copy-start.1 = (bf16[1,64,256]{2,1,0:T(8,128)(2,1)S(1)}, bf16[1,64,256]{2,1,0:T(8,128)(2,1)}, u32[]{:S(2)}) copy-start(bf16[1,64,256]{2,1,0:T(8,128)(2,1)} %param.21) | copy-start | bytes 98308
  40.8 72.7 %copy-start.2 = (s32[1,64,1]{1,2,0:T(1,128)S(1)}, s32[1,64,1]{1,2,0:T(1,128)}, u32[]{:S(2)}) copy-start(s32[1,64,1]{1,2,0:T(1,128)} %param.22) | copy-start | bytes 772
  41.1 7.3 %collective-permute-start.1 = (bf16[8,136,128]{2,1,0:T(8,128)(2,1)S(1)}, bf16[8,136,128]{2,1,0:T(8,128)(2,1)S(1)}, u32[]{:S(2)}, u32[]{:S(2)}) collective-permute-start(bf16[8,136,128]{2,1,0:T(8,128)(2,1)S(1)} %get-tuple-element.11), channel_id=1, source_target_pairs={{0,24},{32,56},{64,88},{96,120},{128,152},{160,184},{192,216},{224... | collective-permute-start | bytes 835592 | tf_op jit(solution)/shard_map/ppermute | solution.py:330
  49.2 25.0 %all-to-all-start.1 = ((bf16[8,136,128]{2,1,0:T(8,128)(2,1)}), bf16[8,136,128]{2,1,0:T(8,128)(2,1)S(1)}, u32[]{:S(2)}, u32[]{:S(2)}) async-start(bf16[8,136,128]{2,1,0:T(8,128)(2,1)} %add.1), calls=%async_computation.1 | async-start | bytes 557056 | tf_op jit(solution)/shard_map/all_to_all | solution.py:245

commit v9 on v8

--- a/solution.py
+++ b/solution.py
@@ -197,7 +197,8 @@
     keep_ref[...] = sum(parts_ref[s, pair].astype(F32) for s in members)
 
 
-def add_kernel(keep_ref, got_ref, out_ref):
+def add_kernel(gain_ref, keep_ref, got_ref, out_ref, spread_ref):
+    spread_ref[...] = jnp.full(spread_ref.shape, gain_ref[0], F32)
     out_ref[...] = (keep_ref[...] + got_ref[...].astype(F32)).astype(BF16)
 
 
@@ -210,7 +211,7 @@
         coadded = summed[h * rows : (h + 1) * rows] / column
         out_ref[:, part] = coadded
         for b in range(scaled_ref.shape[0]):
-            scaled_ref[b, :, part] = (gain_ref[0] * coadded).astype(BF16)
+            scaled_ref[b, :, part] = (gain_ref[0:1, :] * coadded).astype(BF16)
         asked_ref[:, part] = summed[2 * rows + 1 + h : 2 * rows + 2 + h]
 
 
@@ -320,24 +321,24 @@
         name="split",
         compiler_params=grant(8),
     )(me, along_x)
-    partial = pl.pallas_call(
+    partial, gain = pl.pallas_call(
         add_kernel,
-        out_shape=SDS((depth, high, 128), BF16),
-        in_specs=[VM, VM],
-        out_specs=VM,
+        out_shape=(SDS((depth, high, 128), BF16), SDS((8, 128), F32)),
+        in_specs=[SM, VM, VM],
+        out_specs=(VM, VM),
         name="add",
         compiler_params=grant(8),
-    )(keep, lax.ppermute(send, "sky", cross))
+    )(gains, keep, lax.ppermute(send, "sky", cross))
     along_z = exchange(partial, far)
 
     coadded, scaled, asked = pl.pallas_call(
         coadd_kernel,
         out_shape=(SDS((rows, cols), F32), SDS((band, rows, cols), BF16), SDS((1, cols), F32)),
-        in_specs=[VM, SM],
+        in_specs=[VM, VM],
         out_specs=(VM, VM, VM),
         name="coadd",
         compiler_params=grant(4),
-    )(along_z, gains)
+    )(along_z, gain)
     bands = exchange(scaled, None, "band")
     detection, picked = pl.pallas_call(
         detect_kernel,

time: 115 us -> 114 us (level)
  blocking collectives: 59.8 us -> 84.5 us
  waiting for transfers between devices: 22.5 us -> 4.72 us
  starting transfers between devices: 17.8 us -> 10.7 us
    all_to_all x3 -> x4, blocking collectives: 59.8 us -> 84.5 us  [exchange(): lax.all_to_all(value, axis, split_axis=0, concat_axis=0, tiled=True, axis...]
    all_to_all x1 -> x0, waiting for transfers between devices: 17.1 us -> none  [exchange(): lax.all_to_all(value, axis, split_axis=0, concat_axis=0, tiled=True, axis...]
    all_to_all x1 -> x0, starting transfers between devices: 7.17 us -> none  [exchange(): lax.all_to_all(value, axis, split_axis=0, concat_axis=0, tiled=True, axis...]
  transfers between devices with their start and end apart: 3 -> 2, of which waited for: 2 -> 1; matrix products, arithmetic and copies ran while one was open for 0% -> 0% of each run, Pallas kernels for 1% -> 1%
where the time goes in v9:
time: 114 us; the launch traced here: 113 us
  blocking collectives  84.5 us (74%)
  Pallas kernels  10.7 us (9%)
  starting transfers between devices  10.7 us (9%)
  waiting for transfers between devices  4.72 us (4%)
  between operations  1.37 us (1%)
  local copies, waits for them, and re-layouts  1.34 us (1%)
    all_to_all x4, blocking collectives, exchange(): lax.all_to_all(value, axis, split_axis=0, concat_axis=0, tiled=True, axis...  84.5 us
    ppermute x1, starting transfers between devices, per_device(): other = lax.ppermute(matched, 'sky', partners)  8.75 us
    pallas_call x1, Pallas kernels, per_device(): pl.pallas_call(match_kernel, out_shape=SDS((n + 1, th, cols), BF16), in_s...  5.01 us
    ppermute x1, waiting for transfers between devices, per_device(): lax.ppermute(send, 'sky', cross)  4.72 us
  transfers between devices with their start and end apart: 2, of which 1 were waited for; matrix products, arithmetic and copies ran while one was open for 0% of the time, Pallas kernels for 1%

profile of v9, /device:TPU:1, one launch (start us, length us, event | category | flops | bytes accessed | tf_op | source)
XLA Modules:
  0.0 113.3 jit_solution(5564433585933790398)
XLA Ops:
  0.6 5.0 %match.1.m_ref = bf16[65,32,256]{2,1,0:T(8,128)(2,1)} custom-call(bf16[2048,256]{1,0:T(8,128)(2,1)} %bitcast.16, bf16[5,64]{1,0:T(8,128)(2,1)} %bitcast.17, bf16[5,41]{1,0:T(8,128)(2,1)} %bitcast.18, bf16[5,41]{1,0:T(8,128)(2,1)} %bitcast.19, s32[1,64]{1,0:T(1,128)} %bitcast.20, s32[1,64]{1,0:T(1,128)} %refs_5_.1, s32[1,64]{1,0:T(1,128)} %refs_6_.1, ...), custom_call_target="tpu_custom_call" | custom-call | tf_op jit(solution)/shard_map/match/pallas_call | solution.py:275
  5.7 8.7 %collective-permute-start = (bf16[65,32,256]{2,1,0:T(8,128)(2,1)}, bf16[65,32,256]{2,1,0:T(8,128)(2,1)S(1)}, u32[]{:S(2)}, u32[]{:S(2)}) collective-permute-start(bf16[65,32,256]{2,1,0:T(8,128)(2,1)} %match.1.m_ref), channel_id=1, source_target_pairs={{0,4},{4,0},{8,12},{12,8},{16,20},{20,16},{24,28},{28,24},{32,36},... | collective-permute-start | bytes 3194888 | tf_op jit(solution)/shard_map/ppermute | solution.py:293
  14.4 0.0 copy-start
  14.4 1.2 %copy-done = bf16[65,32,256]{2,1,0:T(8,128)(2,1)S(1)} copy-done((bf16[65,32,256]{2,1,0:T(8,128)(2,1)S(1)}, bf16[65,32,256]{2,1,0:T(8,128)(2,1)}, u32[]{:S(2)}) %copy-start) | copy-done | bytes 1064984
  15.6 1.4 %place_own.1.own_ref = f32[65,136,128]{2,1,0:T(8,128)S(1)} custom-call(s32[1]{0:T(128)} %bitcast.me_ref, bf16[65,32,256]{2,1,0:T(8,128)(2,1)S(1)} %copy-done), custom_call_target="tpu_custom_call" | custom-call | tf_op jit(solution)/shard_map/place_own/pallas_call | solution.py:296
  17.1 0.0 collective-permute-done.o_ref
  17.1 1.8 %place_other.1 = bf16[64,136,128]{2,1,0:T(8,128)(2,1)S(1)} custom-call(s32[1]{0:T(128)} %bitcast.me_ref, bf16[65,32,256]{2,1,0:T(8,128)(2,1)S(1)} %collective-permute-done.o_ref, f32[65,136,128]{2,1,0:T(8,128)S(1)} %place_own.1.own_ref), custom_call_target="tpu_custom_call" | custom-call | tf_op jit(solution)/shard_map/place_other/pallas_call | solution.py:305
  18.9 21.9 %all_to_all.20 = bf16[64,136,128]{2,1,0:T(8,128)(2,1)S(1)} all-to-all(bf16[64,136,128]{2,1,0:T(8,128)(2,1)S(1)} %place_other.1), channel_id=1, replica_groups={{0,8,32,40},{24,16,56,48},{64,72,96,104},{88,80,120,112},{128,136,160,1..., dimensions={0} | all-to-all | bytes 4456448 | tf_op jit(solution)/shard_map/all_to_all | solution.py:246
  40.8 0.0 copy-start.1
  40.8 0.0 copy-start.2
  40.8 0.3 split.1
  41.1 1.9 %collective-permute-start.1 = (bf16[8,136,128]{2,1,0:T(8,128)(2,1)S(1)}, bf16[8,136,128]{2,1,0:T(8,128)(2,1)S(1)}, u32[]{:S(2)}, u32[]{:S(2)}) collective-permute-start(bf16[8,136,128]{2,1,0:T(8,128)(2,1)S(1)} %get-tuple-element.13), channel_id=1, source_target_pairs={{0,24},{32,56},{64,88},{96,120},{128,152},{160,184},{192,216},{224... | collective-permute-start | bytes 835592 | tf_op jit(solution)/shard_map/ppermute | solution.py:331
  43.7 4.7 %collective-permute-done.1.got_ref = bf16[8,136,128]{2,1,0:T(8,128)(2,1)S(1)} collective-permute-done((bf16[8,136,128]{2,1,0:T(8,128)(2,1)S(1)}, bf16[8,136,128]{2,1,0:T(8,128)(2,1)S(1)}, u32[]{:S(2)}, u32[]{:S(2)}) %collective-permute-start.1) | collective-permute-done | bytes 278560 | tf_op jit(solution)/shard_map/ppermute | solution.py:331
  48.4 26.5 %all_to_all.21.parts_ref = bf16[8,136,128]{2,1,0:T(8,128)(2,1)S(1)} all-to-all(bf16[8,136,128]{2,1,0:T(8,128)(2,1)S(1)} %get-tuple-element.14), channel_id=1, replica_groups={{0,64,128,192,256,320,384,448},{4,68,132,196,260,324,388,452},{8,72,136..., dimensions={0} | all-to-all | bytes 557056 | tf_op jit(solution)/shard_map/all_to_all | solution.py:246
  74.9 0.7 coadd.1
  75.7 8.8 %all_to_all.22.bands_ref = bf16[4,64,256]{2,1,0:T(8,128)(2,1)S(1)} all-to-all(bf16[4,64,256]{2,1,0:T(8,128)(2,1)S(1)} %get-tuple-element.17), channel_id=1, replica_groups=mesh['sky'=128,'band'=4] {'band'}, dimensions={0} | all-to-all | bytes 262144 | tf_op jit(solution)/shard_map/all_to_all | solution.py:246
  84.5 0.7 detect.1
  85.1 0.1 reshape.20
  85.2 27.4 %all_to_all.23 = bf16[128,2,256]{2,1,0:T(2,128)(2,1)S(1)} all-to-all(bf16[128,2,256]{2,1,0:T(2,128)(2,1)S(1)} %reshape.20), channel_id=1, replica_groups=mesh['sky'=128,'band'=4] {'sky'}, dimensions={0} | all-to-all | bytes 262144 | tf_op jit(solution)/shard_map/all_to_all | solution.py:246
  112.5 0.1 reshape.21.rows_ref
  112.6 0.0 copy-done.1
  112.6 0.0 copy-done.2
  112.6 0.7 flux.1
  (1 shorter events, 0.0 us)
Async XLA Ops:
  5.7 11.4 %collective-permute-start = (bf16[65,32,256]{2,1,0:T(8,128)(2,1)}, bf16[65,32,256]{2,1,0:T(8,128)(2,1)S(1)}, u32[]{:S(2)}, u32[]{:S(2)}) collective-permute-start(bf16[65,32,256]{2,1,0:T(8,128)(2,1)} %match.1.m_ref), channel_id=1, source_target_pairs={{0,4},{4,0},{8,12},{12,8},{16,20},{20,16},{24,28},{28,24},{32,36},... | collective-permute-start | bytes 3194888 | tf_op jit(solution)/shard_map/ppermute | solution.py:293
  14.4 1.2 %copy-start = (bf16[65,32,256]{2,1,0:T(8,128)(2,1)S(1)}, bf16[65,32,256]{2,1,0:T(8,128)(2,1)}, u32[]{:S(2)}) copy-start(bf16[65,32,256]{2,1,0:T(8,128)(2,1)} %match.1.m_ref) | copy-start | bytes 3194884
  40.8 71.8 %copy-start.1 = (bf16[1,64,256]{2,1,0:T(8,128)(2,1)S(1)}, bf16[1,64,256]{2,1,0:T(8,128)(2,1)}, u32[]{:S(2)}) copy-start(bf16[1,64,256]{2,1,0:T(8,128)(2,1)} %param.21) | copy-start | bytes 98308
  40.8 71.8 %copy-start.2 = (s32[1,64,1]{1,2,0:T(1,128)S(1)}, s32[1,64,1]{1,2,0:T(1,128)}, u32[]{:S(2)}) copy-start(s32[1,64,1]{1,2,0:T(1,128)} %param.22) | copy-start | bytes 772
  41.1 7.3 %collective-permute-start.1 = (bf16[8,136,128]{2,1,0:T(8,128)(2,1)S(1)}, bf16[8,136,128]{2,1,0:T(8,128)(2,1)S(1)}, u32[]{:S(2)}, u32[]{:S(2)}) collective-permute-start(bf16[8,136,128]{2,1,0:T(8,128)(2,1)S(1)} %get-tuple-element.13), channel_id=1, source_target_pairs={{0,24},{32,56},{64,88},{96,120},{128,152},{160,184},{192,216},{224... | collective-permute-start | bytes 835592 | tf_op jit(solution)/shard_map/ppermute | solution.py:331
